TPU v7x, 256 devices: a whole 4x4x8 slice. The times are simulated.
256 devices in a mesh: freq: 4 (over y), mx: 8 (over x, core), my: 8 (over z).
Axes of the slice: x: 4, y: 4, z: 8, core: 2. Of those that a mesh axis runs over, the one named last changes fastest.
Arguments:
- adjoint_rhs: float32 [4, 2, 3, 512, 2048], P('freq', None, None, 'mx', 'my'), may hold values from -4 to 6
- state: bfloat16 [4, 2, 3, 512, 2048], P('freq', None, None, 'mx', 'my'), may hold values from -1.5 to 1.5
- density: float32 [512, 2048], P('mx', 'my'), may hold values from 0.85 to 1
- stiffness: float32 [512, 2048], P('mx', 'my'), may hold values from 1.5 to 4
- mass: float32 [512, 2048], P('mx', 'my'), may hold values from 0.2 to 1
- omega: float32 [4], P('freq'), may hold values from 0.15 to 0.45
- send_rows: int32 [64, 2048], P(('mx', 'my')), may hold values from 0 to 16383, as said below
- recv_rows: int32 [64, 2048], P(('mx', 'my')), may hold values from 0 to 16383, as said below
- mortar_weight: float32 [64, 2048], P(('mx', 'my')), may hold values from 0 to 1.5, as said below
Outputs:
- adjoint: float32 [4, 2, 3, 512, 2048], P('freq', None, None, 'mx', 'my')
- filtered_sensitivity: float32 [512, 2048], P('mx', 'my')
Inputs may be any that keep to these rules, and one draw needn't show every extreme that they name: `send_rows`: a local cell of the sending device; slots past the live count of a device pair hold 0. `recv_rows`: a local cell of the receiving device; empty slots hold 0. Live slots of a pair come first, up to 32 of them. `mortar_weight`: zero exactly in empty slots, at least 0.5 in live ones; every receiving device has a source device with all 32 slots live.
All inputs are finite; a program needn't handle non-finite values.
Results may differ from a plain program's by a relative error of at most 0.0003.
Values may be sent and summed in bfloat16 or wider, within the bound.
A program may use at most 64 MiB of HBM per device.

v0:
```python
import jax
import jax.numpy as jnp
from jax import lax
from jax.sharding import PartitionSpec as P

ITERS = 20


def extended(x, sides, width):
    for axis, dim in sides:
        size, length = (lax.axis_size(axis), x.shape[dim])
        up = [(i, (i + 1) % size) for i in range(size - 1)]
        down = [(j, i) for i, j in up]
        last = lax.slice_in_dim(x, length - width, length, axis=dim)
        first = lax.slice_in_dim(x, 0, width, axis=dim)
        before = lax.ppermute(last, axis, up)
        after = lax.ppermute(first, axis, down)
        x = jnp.concatenate([before, x, after], axis=dim)
    return x


def on_device(
    adjoint_rhs, state, density, stiffness, mass, omega, send_rows, recv_rows, mortar_weight
):
    rows_x, rows_y = density.shape
    cells = rows_x * rows_y
    w = omega[0]
    stiff = density**3 * stiffness
    dstiff = 3.0 * density**2 * stiffness
    rmass = density * mass
    sources = send_rows[0]
    targets = recv_rows[0]
    weights = mortar_weight[0]
    mdiag = jnp.zeros((cells,), jnp.float32).at[targets].add(weights).reshape(rows_x, rows_y)
    real_d = 4.4 * stiff + 0.3 + mdiag - w * w * rmass
    imag_d = 0.2 * w * (stiff + rmass)
    den = real_d * real_d + imag_d * imag_d
    rhs = adjoint_rhs.reshape(6, rows_x, rows_y)

    def mortar(field):
        sent = field.reshape(6, cells)[:, sources]
        got = lax.all_to_all(sent, ("mx", "my"), split_axis=1, concat_axis=1, tiled=True)
        added = jnp.zeros((6, cells), jnp.float32).at[:, targets].add(got * weights)
        return added.reshape(6, rows_x, rows_y)

    def sweep(step, field):
        padded = extended(field, (("mx", 1), ("my", 2)), 1)
        beside = (
            padded[:, 2:, 1:-1] + padded[:, :-2, 1:-1] + padded[:, 1:-1, 2:] + padded[:, 1:-1, :-2]
        )
        h = rhs + stiff * beside + mortar(field)
        new_re = (h[:3] * real_d + h[3:] * imag_d) / den
        new_im = (h[3:] * real_d - h[:3] * imag_d) / den
        return jnp.concatenate([new_re, new_im], axis=0)

    field = lax.fori_loop(0, ITERS, sweep, jnp.zeros((6, rows_x, rows_y), jnp.float32))
    state_six = state.reshape(6, rows_x, rows_y)
    state_pad = extended(state_six, (("mx", 1), ("my", 2)), 1).astype(jnp.float32)
    u = state_six.astype(jnp.float32)
    nb = (
        state_pad[:, 2:, 1:-1]
        + state_pad[:, :-2, 1:-1]
        + state_pad[:, 1:-1, 2:]
        + state_pad[:, 1:-1, :-2]
    )
    da = 4.4 * dstiff - w * w * mass
    db = 0.2 * w * (dstiff + mass)
    t_re = da * u[:3] - db * u[3:] - dstiff * nb[:3]
    t_im = da * u[3:] + db * u[:3] - dstiff * nb[3:]
    sens = -jnp.sum(field[:3] * t_re - field[3:] * t_im, axis=0)
    total = lax.psum(sens, "freq")
    weighted = extended(density * total, (("mx", 0), ("my", 1)), 1)
    filt = weighted[1:-1, 1:-1]
    filt = filt + 0.5 * (
        weighted[2:, 1:-1] + weighted[:-2, 1:-1] + weighted[1:-1, 2:] + weighted[1:-1, :-2]
    )
    filt = filt + 0.25 * (
        weighted[2:, 2:] + weighted[:-2, :-2] + weighted[2:, :-2] + weighted[:-2, 2:]
    )
    return (field.reshape(1, 2, 3, rows_x, rows_y), filt / (4.0 * density))


def solution(mesh):
    return jax.shard_map(
        on_device,
        mesh=mesh,
        in_specs=(
            P("freq", None, None, "mx", "my"),
            P("freq", None, None, "mx", "my"),
            P("mx", "my"),
            P("mx", "my"),
            P("mx", "my"),
            P("freq"),
            P(("mx", "my"), None),
            P(("mx", "my"), None),
            P(("mx", "my"), None),
        ),
        out_specs=(P("freq", None, None, "mx", "my"), P("mx", "my")),
        check_vma=False,
    )
```

profile of v0, /device:TPU:1, one launch (start us, length us, event | category | flops | bytes accessed | tf_op | source)
XLA Modules:
  0.0 1373.5 jit_solution(1580240488645792618)
XLA Ops:
  16.4 11.6 scatter_custom_fusion.1
  41.2 1256.1 %while.10 = (s32[]{:T(128)}, f32[6,64,256]{2,1,0:T(8,128)S(1)}, f32[64,256]{1,0:T(8,128)S(1)}, f32[6,64,256]{2,1,0:T(8,128)}, s32[2048]{0:T(1024)}, /*index=5*/s...) while((s32[]{:T(128)}, f32[6,64,256]{2,1,0:T(8,128)S(1)}, ...), condition=%wide.region_3.0_spmd, body=%wide.region_1.0_spmd.sunk | while | flops 2109442 | bytes 9095261 | solution.py:56
  46.0 8.8 gather_fusion
  56.1 14.4 %all-to-all-start = ((f32[64,1,192]{2,1,0:T(1,128)}), f32[64,1,192]{2,1,0:T(1,128)S(1)}, u32[]{:S(2)}, u32[]{:S(2)}) async-start(f32[64,1,192]{2,1,0:T(1,128)} %reshape.136), calls=%async_computation | async-start | bytes 131072 | tf_op jit(solution)/shard_map/while/body/eval_jaxpr/all_to_all | solution.py:42
  83.6 15.2 %scatter_custom_fusion.7 = f32[6,16384]{0,1:T(8,128)} fusion(s32[2048]{0:T(1024)S(1)} %bitcast.65, f32[2048,6]{1,0:T(8,128)S(1)} %copy.34, f32[]{:T(128)} %constant.21.clone.1..sunk), kind=kCustom, calls=%fused_computation.3.clone.1 | custom fusion | flops 12288 | bytes 393220 | tf_op jit(solution)/shard_map/while/body/eval_jaxpr/scatter-add | solution.py:43
  98.8 5.3 copy.35
  109.4 8.8 gather_fusion
  119.5 13.7 all-to-all-start
  146.3 15.2 %scatter_custom_fusion.7 = f32[6,16384]{0,1:T(8,128)} fusion(s32[2048]{0:T(1024)S(1)} %bitcast.65, f32[2048,6]{1,0:T(8,128)S(1)} %copy.34, f32[]{:T(128)} %constant.21.clone.1..sunk), kind=kCustom, calls=%fused_computation.3.clone.1 | custom fusion | flops 12288 | bytes 393220 | tf_op jit(solution)/shard_map/while/body/eval_jaxpr/scatter-add | solution.py:43
  172.2 8.8 gather_fusion
  182.3 13.7 all-to-all-start
  209.1 15.2 %scatter_custom_fusion.7 = f32[6,16384]{0,1:T(8,128)} fusion(s32[2048]{0:T(1024)S(1)} %bitcast.65, f32[2048,6]{1,0:T(8,128)S(1)} %copy.34, f32[]{:T(128)} %constant.21.clone.1..sunk), kind=kCustom, calls=%fused_computation.3.clone.1 | custom fusion | flops 12288 | bytes 393220 | tf_op jit(solution)/shard_map/while/body/eval_jaxpr/scatter-add | solution.py:43
  234.9 8.8 gather_fusion
  245.0 13.7 all-to-all-start
  271.9 15.2 %scatter_custom_fusion.7 = f32[6,16384]{0,1:T(8,128)} fusion(s32[2048]{0:T(1024)S(1)} %bitcast.65, f32[2048,6]{1,0:T(8,128)S(1)} %copy.34, f32[]{:T(128)} %constant.21.clone.1..sunk), kind=kCustom, calls=%fused_computation.3.clone.1 | custom fusion | flops 12288 | bytes 393220 | tf_op jit(solution)/shard_map/while/body/eval_jaxpr/scatter-add | solution.py:43
  297.7 8.8 gather_fusion
  307.8 13.7 all-to-all-start
  334.6 15.2 %scatter_custom_fusion.7 = f32[6,16384]{0,1:T(8,128)} fusion(s32[2048]{0:T(1024)S(1)} %bitcast.65, f32[2048,6]{1,0:T(8,128)S(1)} %copy.34, f32[]{:T(128)} %constant.21.clone.1..sunk), kind=kCustom, calls=%fused_computation.3.clone.1 | custom fusion | flops 12288 | bytes 393220 | tf_op jit(solution)/shard_map/while/body/eval_jaxpr/scatter-add | solution.py:43
  360.5 8.8 gather_fusion
  370.6 13.7 all-to-all-start
  397.4 15.2 %scatter_custom_fusion.7 = f32[6,16384]{0,1:T(8,128)} fusion(s32[2048]{0:T(1024)S(1)} %bitcast.65, f32[2048,6]{1,0:T(8,128)S(1)} %copy.34, f32[]{:T(128)} %constant.21.clone.1..sunk), kind=kCustom, calls=%fused_computation.3.clone.1 | custom fusion | flops 12288 | bytes 393220 | tf_op jit(solution)/shard_map/while/body/eval_jaxpr/scatter-add | solution.py:43
  423.3 8.8 gather_fusion
  433.4 13.7 all-to-all-start
  460.2 15.2 %scatter_custom_fusion.7 = f32[6,16384]{0,1:T(8,128)} fusion(s32[2048]{0:T(1024)S(1)} %bitcast.65, f32[2048,6]{1,0:T(8,128)S(1)} %copy.34, f32[]{:T(128)} %constant.21.clone.1..sunk), kind=kCustom, calls=%fused_computation.3.clone.1 | custom fusion | flops 12288 | bytes 393220 | tf_op jit(solution)/shard_map/while/body/eval_jaxpr/scatter-add | solution.py:43
  486.0 8.8 gather_fusion
  496.1 13.7 all-to-all-start
  523.0 15.2 %scatter_custom_fusion.7 = f32[6,16384]{0,1:T(8,128)} fusion(s32[2048]{0:T(1024)S(1)} %bitcast.65, f32[2048,6]{1,0:T(8,128)S(1)} %copy.34, f32[]{:T(128)} %constant.21.clone.1..sunk), kind=kCustom, calls=%fused_computation.3.clone.1 | custom fusion | flops 12288 | bytes 393220 | tf_op jit(solution)/shard_map/while/body/eval_jaxpr/scatter-add | solution.py:43
  548.8 8.8 gather_fusion
  558.9 13.7 all-to-all-start
  585.7 15.2 %scatter_custom_fusion.7 = f32[6,16384]{0,1:T(8,128)} fusion(s32[2048]{0:T(1024)S(1)} %bitcast.65, f32[2048,6]{1,0:T(8,128)S(1)} %copy.34, f32[]{:T(128)} %constant.21.clone.1..sunk), kind=kCustom, calls=%fused_computation.3.clone.1 | custom fusion | flops 12288 | bytes 393220 | tf_op jit(solution)/shard_map/while/body/eval_jaxpr/scatter-add | solution.py:43
  611.6 8.8 gather_fusion
  621.7 13.7 all-to-all-start
  648.5 15.2 %scatter_custom_fusion.7 = f32[6,16384]{0,1:T(8,128)} fusion(s32[2048]{0:T(1024)S(1)} %bitcast.65, f32[2048,6]{1,0:T(8,128)S(1)} %copy.34, f32[]{:T(128)} %constant.21.clone.1..sunk), kind=kCustom, calls=%fused_computation.3.clone.1 | custom fusion | flops 12288 | bytes 393220 | tf_op jit(solution)/shard_map/while/body/eval_jaxpr/scatter-add | solution.py:43
  674.3 8.8 gather_fusion
  684.4 13.7 all-to-all-start
  711.3 15.2 %scatter_custom_fusion.7 = f32[6,16384]{0,1:T(8,128)} fusion(s32[2048]{0:T(1024)S(1)} %bitcast.65, f32[2048,6]{1,0:T(8,128)S(1)} %copy.34, f32[]{:T(128)} %constant.21.clone.1..sunk), kind=kCustom, calls=%fused_computation.3.clone.1 | custom fusion | flops 12288 | bytes 393220 | tf_op jit(solution)/shard_map/while/body/eval_jaxpr/scatter-add | solution.py:43
  737.1 8.8 gather_fusion
  747.2 13.7 all-to-all-start
  774.0 15.2 %scatter_custom_fusion.7 = f32[6,16384]{0,1:T(8,128)} fusion(s32[2048]{0:T(1024)S(1)} %bitcast.65, f32[2048,6]{1,0:T(8,128)S(1)} %copy.34, f32[]{:T(128)} %constant.21.clone.1..sunk), kind=kCustom, calls=%fused_computation.3.clone.1 | custom fusion | flops 12288 | bytes 393220 | tf_op jit(solution)/shard_map/while/body/eval_jaxpr/scatter-add | solution.py:43
  799.9 8.8 gather_fusion
  810.0 13.7 all-to-all-start
  836.8 15.2 %scatter_custom_fusion.7 = f32[6,16384]{0,1:T(8,128)} fusion(s32[2048]{0:T(1024)S(1)} %bitcast.65, f32[2048,6]{1,0:T(8,128)S(1)} %copy.34, f32[]{:T(128)} %constant.21.clone.1..sunk), kind=kCustom, calls=%fused_computation.3.clone.1 | custom fusion | flops 12288 | bytes 393220 | tf_op jit(solution)/shard_map/while/body/eval_jaxpr/scatter-add | solution.py:43
  862.7 8.8 gather_fusion
  872.8 13.7 all-to-all-start
  899.6 15.2 %scatter_custom_fusion.7 = f32[6,16384]{0,1:T(8,128)} fusion(s32[2048]{0:T(1024)S(1)} %bitcast.65, f32[2048,6]{1,0:T(8,128)S(1)} %copy.34, f32[]{:T(128)} %constant.21.clone.1..sunk), kind=kCustom, calls=%fused_computation.3.clone.1 | custom fusion | flops 12288 | bytes 393220 | tf_op jit(solution)/shard_map/while/body/eval_jaxpr/scatter-add | solution.py:43
  925.4 8.8 gather_fusion
  935.5 13.7 all-to-all-start
  962.4 15.2 %scatter_custom_fusion.7 = f32[6,16384]{0,1:T(8,128)} fusion(s32[2048]{0:T(1024)S(1)} %bitcast.65, f32[2048,6]{1,0:T(8,128)S(1)} %copy.34, f32[]{:T(128)} %constant.21.clone.1..sunk), kind=kCustom, calls=%fused_computation.3.clone.1 | custom fusion | flops 12288 | bytes 393220 | tf_op jit(solution)/shard_map/while/body/eval_jaxpr/scatter-add | solution.py:43
  988.2 8.8 gather_fusion
  998.3 13.7 all-to-all-start
  1025.1 15.2 %scatter_custom_fusion.7 = f32[6,16384]{0,1:T(8,128)} fusion(s32[2048]{0:T(1024)S(1)} %bitcast.65, f32[2048,6]{1,0:T(8,128)S(1)} %copy.34, f32[]{:T(128)} %constant.21.clone.1..sunk), kind=kCustom, calls=%fused_computation.3.clone.1 | custom fusion | flops 12288 | bytes 393220 | tf_op jit(solution)/shard_map/while/body/eval_jaxpr/scatter-add | solution.py:43
  1051.0 8.8 gather_fusion
  1061.1 13.7 all-to-all-start
  1087.9 15.2 %scatter_custom_fusion.7 = f32[6,16384]{0,1:T(8,128)} fusion(s32[2048]{0:T(1024)S(1)} %bitcast.65, f32[2048,6]{1,0:T(8,128)S(1)} %copy.34, f32[]{:T(128)} %constant.21.clone.1..sunk), kind=kCustom, calls=%fused_computation.3.clone.1 | custom fusion | flops 12288 | bytes 393220 | tf_op jit(solution)/shard_map/while/body/eval_jaxpr/scatter-add | solution.py:43
  1113.7 8.8 gather_fusion
  1123.8 13.7 all-to-all-start
  1150.7 15.2 %scatter_custom_fusion.7 = f32[6,16384]{0,1:T(8,128)} fusion(s32[2048]{0:T(1024)S(1)} %bitcast.65, f32[2048,6]{1,0:T(8,128)S(1)} %copy.34, f32[]{:T(128)} %constant.21.clone.1..sunk), kind=kCustom, calls=%fused_computation.3.clone.1 | custom fusion | flops 12288 | bytes 393220 | tf_op jit(solution)/shard_map/while/body/eval_jaxpr/scatter-add | solution.py:43
  1176.5 8.8 gather_fusion
  1186.6 13.7 all-to-all-start
  1213.4 15.2 %scatter_custom_fusion.7 = f32[6,16384]{0,1:T(8,128)} fusion(s32[2048]{0:T(1024)S(1)} %bitcast.65, f32[2048,6]{1,0:T(8,128)S(1)} %copy.34, f32[]{:T(128)} %constant.21.clone.1..sunk), kind=kCustom, calls=%fused_computation.3.clone.1 | custom fusion | flops 12288 | bytes 393220 | tf_op jit(solution)/shard_map/while/body/eval_jaxpr/scatter-add | solution.py:43
  1239.3 8.8 gather_fusion
  1249.4 13.7 all-to-all-start
  1276.2 15.2 %scatter_custom_fusion.7 = f32[6,16384]{0,1:T(8,128)} fusion(s32[2048]{0:T(1024)S(1)} %bitcast.65, f32[2048,6]{1,0:T(8,128)S(1)} %copy.34, f32[]{:T(128)} %constant.21.clone.1..sunk), kind=kCustom, calls=%fused_computation.3.clone.1 | custom fusion | flops 12288 | bytes 393220 | tf_op jit(solution)/shard_map/while/body/eval_jaxpr/scatter-add | solution.py:43
  1299.3 49.0 %all-reduce.2.cloned.1.call-done = f32[64,256]{1,0:T(8,128)} async-done(((f32[64,256]{1,0:T(8,128)}), f32[64,256]{1,0:T(8,128)}) %all-reduce.2.cloned.1.call-update) | async-done | bytes 65552 | tf_op jit(solution)/shard_map/psum | solution.py:71
  (782 shorter events, 531.9 us)
Async XLA Ops:
  7.2 1341.1 %all-reduce.2.cloned.1.call-start = ((), (), s32[]{:S(2)}) async-start(), calls=%async_computation.1 | async-start | bytes 131072 | tf_op jit(solution)/shard_map/psum | solution.py:71
  8.0 22.6 %collective-permute-start.5 = (bf16[6,1,256]{2,1,0:T(2,128)(2,1)S(1)}, bf16[6,1,256]{2,1,0:T(2,128)(2,1)S(1)}, u32[]{:S(2)}, u32[]{:S(2)}) collective-permute-start(bf16[6,1,256]{2,1,0:T(2,128)(2,1)S(1)} %get-tuple-element.104), channel_id=1, source_target_pairs={{8,0},{16,8},{24,16},{32,24},{40,32},{48,40},{56,48},{9,1},{17,9},... | collective-permute-start | bytes 9224 | tf_op jit(solution)/shard_map/ppermute | solution.py:17
  13.1 17.5 %collective-permute-start.4 = (bf16[6,1,256]{2,1,0:T(2,128)(2,1)S(1)}, bf16[6,1,256]{2,1,0:T(2,128)(2,1)S(1)}, u32[]{:S(2)}, u32[]{:S(2)}) collective-permute-start(bf16[6,1,256]{2,1,0:T(2,128)(2,1)S(1)} %get-tuple-element.103), channel_id=1, source_target_pairs={{0,8},{8,16},{16,24},{24,32},{32,40},{40,48},{48,56},{1,9},{9,17},... | collective-permute-start | bytes 9224 | tf_op jit(solution)/shard_map/ppermute | solution.py:16
  56.1 25.5 %all-to-all-start = ((f32[64,1,192]{2,1,0:T(1,128)}), f32[64,1,192]{2,1,0:T(1,128)S(1)}, u32[]{:S(2)}, u32[]{:S(2)}) async-start(f32[64,1,192]{2,1,0:T(1,128)} %reshape.136), calls=%async_computation | async-start | bytes 131072 | tf_op jit(solution)/shard_map/while/body/eval_jaxpr/all_to_all | solution.py:42
  77.0 27.1 %collective-permute-start.2 = (f32[6,66,1]{2,1,0:T(8,128)S(1)}, f32[6,66,1]{2,1,0:T(8,128)S(1)}, u32[]{:S(2)}, u32[]{:S(2)}) collective-permute-start(f32[6,66,1]{2,1,0:T(8,128)S(1)} %get-tuple-element.180), channel_id=1, source_target_pairs={{0,1},{1,2},{2,3},{3,4},{4,5},{5,6},{6,7},{8,9},{9,10},{10,11},{11... | collective-permute-start | bytes 4760 | tf_op jit(solution)/shard_map/while/body/eval_jaxpr/ppermute | solution.py:16
  80.2 23.8 %collective-permute-start.3 = (f32[6,66,1]{2,1,0:T(8,128)S(1)}, f32[6,66,1]{2,1,0:T(8,128)S(1)}, u32[]{:S(2)}, u32[]{:S(2)}) collective-permute-start(f32[6,66,1]{2,1,0:T(8,128)S(1)} %get-tuple-element.181), channel_id=1, source_target_pairs={{1,0},{2,1},{3,2},{4,3},{5,4},{6,5},{7,6},{9,8},{10,9},{11,10},{12... | collective-permute-start | bytes 4760 | tf_op jit(solution)/shard_map/while/body/eval_jaxpr/ppermute | solution.py:17
  119.5 24.8 %all-to-all-start = ((f32[64,1,192]{2,1,0:T(1,128)}), f32[64,1,192]{2,1,0:T(1,128)S(1)}, u32[]{:S(2)}, u32[]{:S(2)}) async-start(f32[64,1,192]{2,1,0:T(1,128)} %reshape.136), calls=%async_computation | async-start | bytes 131072 | tf_op jit(solution)/shard_map/while/body/eval_jaxpr/all_to_all | solution.py:42
  139.7 27.1 %collective-permute-start.2 = (f32[6,66,1]{2,1,0:T(8,128)S(1)}, f32[6,66,1]{2,1,0:T(8,128)S(1)}, u32[]{:S(2)}, u32[]{:S(2)}) collective-permute-start(f32[6,66,1]{2,1,0:T(8,128)S(1)} %get-tuple-element.180), channel_id=1, source_target_pairs={{0,1},{1,2},{2,3},{3,4},{4,5},{5,6},{6,7},{8,9},{9,10},{10,11},{11... | collective-permute-start | bytes 4760 | tf_op jit(solution)/shard_map/while/body/eval_jaxpr/ppermute | solution.py:16
  143.0 23.8 %collective-permute-start.3 = (f32[6,66,1]{2,1,0:T(8,128)S(1)}, f32[6,66,1]{2,1,0:T(8,128)S(1)}, u32[]{:S(2)}, u32[]{:S(2)}) collective-permute-start(f32[6,66,1]{2,1,0:T(8,128)S(1)} %get-tuple-element.181), channel_id=1, source_target_pairs={{1,0},{2,1},{3,2},{4,3},{5,4},{6,5},{7,6},{9,8},{10,9},{11,10},{12... | collective-permute-start | bytes 4760 | tf_op jit(solution)/shard_map/while/body/eval_jaxpr/ppermute | solution.py:17
  182.3 24.8 %all-to-all-start = ((f32[64,1,192]{2,1,0:T(1,128)}), f32[64,1,192]{2,1,0:T(1,128)S(1)}, u32[]{:S(2)}, u32[]{:S(2)}) async-start(f32[64,1,192]{2,1,0:T(1,128)} %reshape.136), calls=%async_computation | async-start | bytes 131072 | tf_op jit(solution)/shard_map/while/body/eval_jaxpr/all_to_all | solution.py:42
  202.5 27.1 %collective-permute-start.2 = (f32[6,66,1]{2,1,0:T(8,128)S(1)}, f32[6,66,1]{2,1,0:T(8,128)S(1)}, u32[]{:S(2)}, u32[]{:S(2)}) collective-permute-start(f32[6,66,1]{2,1,0:T(8,128)S(1)} %get-tuple-element.180), channel_id=1, source_target_pairs={{0,1},{1,2},{2,3},{3,4},{4,5},{5,6},{6,7},{8,9},{9,10},{10,11},{11... | collective-permute-start | bytes 4760 | tf_op jit(solution)/shard_map/while/body/eval_jaxpr/ppermute | solution.py:16
  205.8 23.8 %collective-permute-start.3 = (f32[6,66,1]{2,1,0:T(8,128)S(1)}, f32[6,66,1]{2,1,0:T(8,128)S(1)}, u32[]{:S(2)}, u32[]{:S(2)}) collective-permute-start(f32[6,66,1]{2,1,0:T(8,128)S(1)} %get-tuple-element.181), channel_id=1, source_target_pairs={{1,0},{2,1},{3,2},{4,3},{5,4},{6,5},{7,6},{9,8},{10,9},{11,10},{12... | collective-permute-start | bytes 4760 | tf_op jit(solution)/shard_map/while/body/eval_jaxpr/ppermute | solution.py:17
  245.0 24.8 %all-to-all-start = ((f32[64,1,192]{2,1,0:T(1,128)}), f32[64,1,192]{2,1,0:T(1,128)S(1)}, u32[]{:S(2)}, u32[]{:S(2)}) async-start(f32[64,1,192]{2,1,0:T(1,128)} %reshape.136), calls=%async_computation | async-start | bytes 131072 | tf_op jit(solution)/shard_map/while/body/eval_jaxpr/all_to_all | solution.py:42
  265.3 27.1 %collective-permute-start.2 = (f32[6,66,1]{2,1,0:T(8,128)S(1)}, f32[6,66,1]{2,1,0:T(8,128)S(1)}, u32[]{:S(2)}, u32[]{:S(2)}) collective-permute-start(f32[6,66,1]{2,1,0:T(8,128)S(1)} %get-tuple-element.180), channel_id=1, source_target_pairs={{0,1},{1,2},{2,3},{3,4},{4,5},{5,6},{6,7},{8,9},{9,10},{10,11},{11... | collective-permute-start | bytes 4760 | tf_op jit(solution)/shard_map/while/body/eval_jaxpr/ppermute | solution.py:16
  268.6 23.8 %collective-permute-start.3 = (f32[6,66,1]{2,1,0:T(8,128)S(1)}, f32[6,66,1]{2,1,0:T(8,128)S(1)}, u32[]{:S(2)}, u32[]{:S(2)}) collective-permute-start(f32[6,66,1]{2,1,0:T(8,128)S(1)} %get-tuple-element.181), channel_id=1, source_target_pairs={{1,0},{2,1},{3,2},{4,3},{5,4},{6,5},{7,6},{9,8},{10,9},{11,10},{12... | collective-permute-start | bytes 4760 | tf_op jit(solution)/shard_map/while/body/eval_jaxpr/ppermute | solution.py:17
  307.8 24.8 %all-to-all-start = ((f32[64,1,192]{2,1,0:T(1,128)}), f32[64,1,192]{2,1,0:T(1,128)S(1)}, u32[]{:S(2)}, u32[]{:S(2)}) async-start(f32[64,1,192]{2,1,0:T(1,128)} %reshape.136), calls=%async_computation | async-start | bytes 131072 | tf_op jit(solution)/shard_map/while/body/eval_jaxpr/all_to_all | solution.py:42
  328.0 27.1 %collective-permute-start.2 = (f32[6,66,1]{2,1,0:T(8,128)S(1)}, f32[6,66,1]{2,1,0:T(8,128)S(1)}, u32[]{:S(2)}, u32[]{:S(2)}) collective-permute-start(f32[6,66,1]{2,1,0:T(8,128)S(1)} %get-tuple-element.180), channel_id=1, source_target_pairs={{0,1},{1,2},{2,3},{3,4},{4,5},{5,6},{6,7},{8,9},{9,10},{10,11},{11... | collective-permute-start | bytes 4760 | tf_op jit(solution)/shard_map/while/body/eval_jaxpr/ppermute | solution.py:16
  331.3 23.8 %collective-permute-start.3 = (f32[6,66,1]{2,1,0:T(8,128)S(1)}, f32[6,66,1]{2,1,0:T(8,128)S(1)}, u32[]{:S(2)}, u32[]{:S(2)}) collective-permute-start(f32[6,66,1]{2,1,0:T(8,128)S(1)} %get-tuple-element.181), channel_id=1, source_target_pairs={{1,0},{2,1},{3,2},{4,3},{5,4},{6,5},{7,6},{9,8},{10,9},{11,10},{12... | collective-permute-start | bytes 4760 | tf_op jit(solution)/shard_map/while/body/eval_jaxpr/ppermute | solution.py:17
  370.6 24.8 %all-to-all-start = ((f32[64,1,192]{2,1,0:T(1,128)}), f32[64,1,192]{2,1,0:T(1,128)S(1)}, u32[]{:S(2)}, u32[]{:S(2)}) async-start(f32[64,1,192]{2,1,0:T(1,128)} %reshape.136), calls=%async_computation | async-start | bytes 131072 | tf_op jit(solution)/shard_map/while/body/eval_jaxpr/all_to_all | solution.py:42
  390.8 27.1 %collective-permute-start.2 = (f32[6,66,1]{2,1,0:T(8,128)S(1)}, f32[6,66,1]{2,1,0:T(8,128)S(1)}, u32[]{:S(2)}, u32[]{:S(2)}) collective-permute-start(f32[6,66,1]{2,1,0:T(8,128)S(1)} %get-tuple-element.180), channel_id=1, source_target_pairs={{0,1},{1,2},{2,3},{3,4},{4,5},{5,6},{6,7},{8,9},{9,10},{10,11},{11... | collective-permute-start | bytes 4760 | tf_op jit(solution)/shard_map/while/body/eval_jaxpr/ppermute | solution.py:16
  394.1 23.8 %collective-permute-start.3 = (f32[6,66,1]{2,1,0:T(8,128)S(1)}, f32[6,66,1]{2,1,0:T(8,128)S(1)}, u32[]{:S(2)}, u32[]{:S(2)}) collective-permute-start(f32[6,66,1]{2,1,0:T(8,128)S(1)} %get-tuple-element.181), channel_id=1, source_target_pairs={{1,0},{2,1},{3,2},{4,3},{5,4},{6,5},{7,6},{9,8},{10,9},{11,10},{12... | collective-permute-start | bytes 4760 | tf_op jit(solution)/shard_map/while/body/eval_jaxpr/ppermute | solution.py:17
  433.4 24.8 %all-to-all-start = ((f32[64,1,192]{2,1,0:T(1,128)}), f32[64,1,192]{2,1,0:T(1,128)S(1)}, u32[]{:S(2)}, u32[]{:S(2)}) async-start(f32[64,1,192]{2,1,0:T(1,128)} %reshape.136), calls=%async_computation | async-start | bytes 131072 | tf_op jit(solution)/shard_map/while/body/eval_jaxpr/all_to_all | solution.py:42
  453.6 27.1 %collective-permute-start.2 = (f32[6,66,1]{2,1,0:T(8,128)S(1)}, f32[6,66,1]{2,1,0:T(8,128)S(1)}, u32[]{:S(2)}, u32[]{:S(2)}) collective-permute-start(f32[6,66,1]{2,1,0:T(8,128)S(1)} %get-tuple-element.180), channel_id=1, source_target_pairs={{0,1},{1,2},{2,3},{3,4},{4,5},{5,6},{6,7},{8,9},{9,10},{10,11},{11... | collective-permute-start | bytes 4760 | tf_op jit(solution)/shard_map/while/body/eval_jaxpr/ppermute | solution.py:16
  456.9 23.8 %collective-permute-start.3 = (f32[6,66,1]{2,1,0:T(8,128)S(1)}, f32[6,66,1]{2,1,0:T(8,128)S(1)}, u32[]{:S(2)}, u32[]{:S(2)}) collective-permute-start(f32[6,66,1]{2,1,0:T(8,128)S(1)} %get-tuple-element.181), channel_id=1, source_target_pairs={{1,0},{2,1},{3,2},{4,3},{5,4},{6,5},{7,6},{9,8},{10,9},{11,10},{12... | collective-permute-start | bytes 4760 | tf_op jit(solution)/shard_map/while/body/eval_jaxpr/ppermute | solution.py:17
  496.1 24.8 %all-to-all-start = ((f32[64,1,192]{2,1,0:T(1,128)}), f32[64,1,192]{2,1,0:T(1,128)S(1)}, u32[]{:S(2)}, u32[]{:S(2)}) async-start(f32[64,1,192]{2,1,0:T(1,128)} %reshape.136), calls=%async_computation | async-start | bytes 131072 | tf_op jit(solution)/shard_map/while/body/eval_jaxpr/all_to_all | solution.py:42
  516.4 27.1 %collective-permute-start.2 = (f32[6,66,1]{2,1,0:T(8,128)S(1)}, f32[6,66,1]{2,1,0:T(8,128)S(1)}, u32[]{:S(2)}, u32[]{:S(2)}) collective-permute-start(f32[6,66,1]{2,1,0:T(8,128)S(1)} %get-tuple-element.180), channel_id=1, source_target_pairs={{0,1},{1,2},{2,3},{3,4},{4,5},{5,6},{6,7},{8,9},{9,10},{10,11},{11... | collective-permute-start | bytes 4760 | tf_op jit(solution)/shard_map/while/body/eval_jaxpr/ppermute | solution.py:16
  519.6 23.8 %collective-permute-start.3 = (f32[6,66,1]{2,1,0:T(8,128)S(1)}, f32[6,66,1]{2,1,0:T(8,128)S(1)}, u32[]{:S(2)}, u32[]{:S(2)}) collective-permute-start(f32[6,66,1]{2,1,0:T(8,128)S(1)} %get-tuple-element.181), channel_id=1, source_target_pairs={{1,0},{2,1},{3,2},{4,3},{5,4},{6,5},{7,6},{9,8},{10,9},{11,10},{12... | collective-permute-start | bytes 4760 | tf_op jit(solution)/shard_map/while/body/eval_jaxpr/ppermute | solution.py:17
  558.9 24.8 %all-to-all-start = ((f32[64,1,192]{2,1,0:T(1,128)}), f32[64,1,192]{2,1,0:T(1,128)S(1)}, u32[]{:S(2)}, u32[]{:S(2)}) async-start(f32[64,1,192]{2,1,0:T(1,128)} %reshape.136), calls=%async_computation | async-start | bytes 131072 | tf_op jit(solution)/shard_map/while/body/eval_jaxpr/all_to_all | solution.py:42
  579.1 27.1 %collective-permute-start.2 = (f32[6,66,1]{2,1,0:T(8,128)S(1)}, f32[6,66,1]{2,1,0:T(8,128)S(1)}, u32[]{:S(2)}, u32[]{:S(2)}) collective-permute-start(f32[6,66,1]{2,1,0:T(8,128)S(1)} %get-tuple-element.180), channel_id=1, source_target_pairs={{0,1},{1,2},{2,3},{3,4},{4,5},{5,6},{6,7},{8,9},{9,10},{10,11},{11... | collective-permute-start | bytes 4760 | tf_op jit(solution)/shard_map/while/body/eval_jaxpr/ppermute | solution.py:16
  582.4 23.8 %collective-permute-start.3 = (f32[6,66,1]{2,1,0:T(8,128)S(1)}, f32[6,66,1]{2,1,0:T(8,128)S(1)}, u32[]{:S(2)}, u32[]{:S(2)}) collective-permute-start(f32[6,66,1]{2,1,0:T(8,128)S(1)} %get-tuple-element.181), channel_id=1, source_target_pairs={{1,0},{2,1},{3,2},{4,3},{5,4},{6,5},{7,6},{9,8},{10,9},{11,10},{12... | collective-permute-start | bytes 4760 | tf_op jit(solution)/shard_map/while/body/eval_jaxpr/ppermute | solution.py:17
  621.7 24.8 %all-to-all-start = ((f32[64,1,192]{2,1,0:T(1,128)}), f32[64,1,192]{2,1,0:T(1,128)S(1)}, u32[]{:S(2)}, u32[]{:S(2)}) async-start(f32[64,1,192]{2,1,0:T(1,128)} %reshape.136), calls=%async_computation | async-start | bytes 131072 | tf_op jit(solution)/shard_map/while/body/eval_jaxpr/all_to_all | solution.py:42
  641.9 27.1 %collective-permute-start.2 = (f32[6,66,1]{2,1,0:T(8,128)S(1)}, f32[6,66,1]{2,1,0:T(8,128)S(1)}, u32[]{:S(2)}, u32[]{:S(2)}) collective-permute-start(f32[6,66,1]{2,1,0:T(8,128)S(1)} %get-tuple-element.180), channel_id=1, source_target_pairs={{0,1},{1,2},{2,3},{3,4},{4,5},{5,6},{6,7},{8,9},{9,10},{10,11},{11... | collective-permute-start | bytes 4760 | tf_op jit(solution)/shard_map/while/body/eval_jaxpr/ppermute | solution.py:16
  645.2 23.8 %collective-permute-start.3 = (f32[6,66,1]{2,1,0:T(8,128)S(1)}, f32[6,66,1]{2,1,0:T(8,128)S(1)}, u32[]{:S(2)}, u32[]{:S(2)}) collective-permute-start(f32[6,66,1]{2,1,0:T(8,128)S(1)} %get-tuple-element.181), channel_id=1, source_target_pairs={{1,0},{2,1},{3,2},{4,3},{5,4},{6,5},{7,6},{9,8},{10,9},{11,10},{12... | collective-permute-start | bytes 4760 | tf_op jit(solution)/shard_map/while/body/eval_jaxpr/ppermute | solution.py:17
  684.4 24.8 %all-to-all-start = ((f32[64,1,192]{2,1,0:T(1,128)}), f32[64,1,192]{2,1,0:T(1,128)S(1)}, u32[]{:S(2)}, u32[]{:S(2)}) async-start(f32[64,1,192]{2,1,0:T(1,128)} %reshape.136), calls=%async_computation | async-start | bytes 131072 | tf_op jit(solution)/shard_map/while/body/eval_jaxpr/all_to_all | solution.py:42
  704.7 27.1 %collective-permute-start.2 = (f32[6,66,1]{2,1,0:T(8,128)S(1)}, f32[6,66,1]{2,1,0:T(8,128)S(1)}, u32[]{:S(2)}, u32[]{:S(2)}) collective-permute-start(f32[6,66,1]{2,1,0:T(8,128)S(1)} %get-tuple-element.180), channel_id=1, source_target_pairs={{0,1},{1,2},{2,3},{3,4},{4,5},{5,6},{6,7},{8,9},{9,10},{10,11},{11... | collective-permute-start | bytes 4760 | tf_op jit(solution)/shard_map/while/body/eval_jaxpr/ppermute | solution.py:16
  708.0 23.8 %collective-permute-start.3 = (f32[6,66,1]{2,1,0:T(8,128)S(1)}, f32[6,66,1]{2,1,0:T(8,128)S(1)}, u32[]{:S(2)}, u32[]{:S(2)}) collective-permute-start(f32[6,66,1]{2,1,0:T(8,128)S(1)} %get-tuple-element.181), channel_id=1, source_target_pairs={{1,0},{2,1},{3,2},{4,3},{5,4},{6,5},{7,6},{9,8},{10,9},{11,10},{12... | collective-permute-start | bytes 4760 | tf_op jit(solution)/shard_map/while/body/eval_jaxpr/ppermute | solution.py:17
  747.2 24.8 %all-to-all-start = ((f32[64,1,192]{2,1,0:T(1,128)}), f32[64,1,192]{2,1,0:T(1,128)S(1)}, u32[]{:S(2)}, u32[]{:S(2)}) async-start(f32[64,1,192]{2,1,0:T(1,128)} %reshape.136), calls=%async_computation | async-start | bytes 131072 | tf_op jit(solution)/shard_map/while/body/eval_jaxpr/all_to_all | solution.py:42
  767.4 27.1 %collective-permute-start.2 = (f32[6,66,1]{2,1,0:T(8,128)S(1)}, f32[6,66,1]{2,1,0:T(8,128)S(1)}, u32[]{:S(2)}, u32[]{:S(2)}) collective-permute-start(f32[6,66,1]{2,1,0:T(8,128)S(1)} %get-tuple-element.180), channel_id=1, source_target_pairs={{0,1},{1,2},{2,3},{3,4},{4,5},{5,6},{6,7},{8,9},{9,10},{10,11},{11... | collective-permute-start | bytes 4760 | tf_op jit(solution)/shard_map/while/body/eval_jaxpr/ppermute | solution.py:16
  770.7 23.8 %collective-permute-start.3 = (f32[6,66,1]{2,1,0:T(8,128)S(1)}, f32[6,66,1]{2,1,0:T(8,128)S(1)}, u32[]{:S(2)}, u32[]{:S(2)}) collective-permute-start(f32[6,66,1]{2,1,0:T(8,128)S(1)} %get-tuple-element.181), channel_id=1, source_target_pairs={{1,0},{2,1},{3,2},{4,3},{5,4},{6,5},{7,6},{9,8},{10,9},{11,10},{12... | collective-permute-start | bytes 4760 | tf_op jit(solution)/shard_map/while/body/eval_jaxpr/ppermute | solution.py:17
  810.0 24.8 %all-to-all-start = ((f32[64,1,192]{2,1,0:T(1,128)}), f32[64,1,192]{2,1,0:T(1,128)S(1)}, u32[]{:S(2)}, u32[]{:S(2)}) async-start(f32[64,1,192]{2,1,0:T(1,128)} %reshape.136), calls=%async_computation | async-start | bytes 131072 | tf_op jit(solution)/shard_map/while/body/eval_jaxpr/all_to_all | solution.py:42
  830.2 27.1 %collective-permute-start.2 = (f32[6,66,1]{2,1,0:T(8,128)S(1)}, f32[6,66,1]{2,1,0:T(8,128)S(1)}, u32[]{:S(2)}, u32[]{:S(2)}) collective-permute-start(f32[6,66,1]{2,1,0:T(8,128)S(1)} %get-tuple-element.180), channel_id=1, source_target_pairs={{0,1},{1,2},{2,3},{3,4},{4,5},{5,6},{6,7},{8,9},{9,10},{10,11},{11... | collective-permute-start | bytes 4760 | tf_op jit(solution)/shard_map/while/body/eval_jaxpr/ppermute | solution.py:16
  833.5 23.8 %collective-permute-start.3 = (f32[6,66,1]{2,1,0:T(8,128)S(1)}, f32[6,66,1]{2,1,0:T(8,128)S(1)}, u32[]{:S(2)}, u32[]{:S(2)}) collective-permute-start(f32[6,66,1]{2,1,0:T(8,128)S(1)} %get-tuple-element.181), channel_id=1, source_target_pairs={{1,0},{2,1},{3,2},{4,3},{5,4},{6,5},{7,6},{9,8},{10,9},{11,10},{12... | collective-permute-start | bytes 4760 | tf_op jit(solution)/shard_map/while/body/eval_jaxpr/ppermute | solution.py:17
  872.8 24.8 %all-to-all-start = ((f32[64,1,192]{2,1,0:T(1,128)}), f32[64,1,192]{2,1,0:T(1,128)S(1)}, u32[]{:S(2)}, u32[]{:S(2)}) async-start(f32[64,1,192]{2,1,0:T(1,128)} %reshape.136), calls=%async_computation | async-start | bytes 131072 | tf_op jit(solution)/shard_map/while/body/eval_jaxpr/all_to_all | solution.py:42
  893.0 27.1 %collective-permute-start.2 = (f32[6,66,1]{2,1,0:T(8,128)S(1)}, f32[6,66,1]{2,1,0:T(8,128)S(1)}, u32[]{:S(2)}, u32[]{:S(2)}) collective-permute-start(f32[6,66,1]{2,1,0:T(8,128)S(1)} %get-tuple-element.180), channel_id=1, source_target_pairs={{0,1},{1,2},{2,3},{3,4},{4,5},{5,6},{6,7},{8,9},{9,10},{10,11},{11... | collective-permute-start | bytes 4760 | tf_op jit(solution)/shard_map/while/body/eval_jaxpr/ppermute | solution.py:16
  896.3 23.8 %collective-permute-start.3 = (f32[6,66,1]{2,1,0:T(8,128)S(1)}, f32[6,66,1]{2,1,0:T(8,128)S(1)}, u32[]{:S(2)}, u32[]{:S(2)}) collective-permute-start(f32[6,66,1]{2,1,0:T(8,128)S(1)} %get-tuple-element.181), channel_id=1, source_target_pairs={{1,0},{2,1},{3,2},{4,3},{5,4},{6,5},{7,6},{9,8},{10,9},{11,10},{12... | collective-permute-start | bytes 4760 | tf_op jit(solution)/shard_map/while/body/eval_jaxpr/ppermute | solution.py:17
  935.5 24.8 %all-to-all-start = ((f32[64,1,192]{2,1,0:T(1,128)}), f32[64,1,192]{2,1,0:T(1,128)S(1)}, u32[]{:S(2)}, u32[]{:S(2)}) async-start(f32[64,1,192]{2,1,0:T(1,128)} %reshape.136), calls=%async_computation | async-start | bytes 131072 | tf_op jit(solution)/shard_map/while/body/eval_jaxpr/all_to_all | solution.py:42
  955.8 27.1 %collective-permute-start.2 = (f32[6,66,1]{2,1,0:T(8,128)S(1)}, f32[6,66,1]{2,1,0:T(8,128)S(1)}, u32[]{:S(2)}, u32[]{:S(2)}) collective-permute-start(f32[6,66,1]{2,1,0:T(8,128)S(1)} %get-tuple-element.180), channel_id=1, source_target_pairs={{0,1},{1,2},{2,3},{3,4},{4,5},{5,6},{6,7},{8,9},{9,10},{10,11},{11... | collective-permute-start | bytes 4760 | tf_op jit(solution)/shard_map/while/body/eval_jaxpr/ppermute | solution.py:16
  959.0 23.8 %collective-permute-start.3 = (f32[6,66,1]{2,1,0:T(8,128)S(1)}, f32[6,66,1]{2,1,0:T(8,128)S(1)}, u32[]{:S(2)}, u32[]{:S(2)}) collective-permute-start(f32[6,66,1]{2,1,0:T(8,128)S(1)} %get-tuple-element.181), channel_id=1, source_target_pairs={{1,0},{2,1},{3,2},{4,3},{5,4},{6,5},{7,6},{9,8},{10,9},{11,10},{12... | collective-permute-start | bytes 4760 | tf_op jit(solution)/shard_map/while/body/eval_jaxpr/ppermute | solution.py:17
  998.3 24.8 %all-to-all-start = ((f32[64,1,192]{2,1,0:T(1,128)}), f32[64,1,192]{2,1,0:T(1,128)S(1)}, u32[]{:S(2)}, u32[]{:S(2)}) async-start(f32[64,1,192]{2,1,0:T(1,128)} %reshape.136), calls=%async_computation | async-start | bytes 131072 | tf_op jit(solution)/shard_map/while/body/eval_jaxpr/all_to_all | solution.py:42
  1018.5 27.1 %collective-permute-start.2 = (f32[6,66,1]{2,1,0:T(8,128)S(1)}, f32[6,66,1]{2,1,0:T(8,128)S(1)}, u32[]{:S(2)}, u32[]{:S(2)}) collective-permute-start(f32[6,66,1]{2,1,0:T(8,128)S(1)} %get-tuple-element.180), channel_id=1, source_target_pairs={{0,1},{1,2},{2,3},{3,4},{4,5},{5,6},{6,7},{8,9},{9,10},{10,11},{11... | collective-permute-start | bytes 4760 | tf_op jit(solution)/shard_map/while/body/eval_jaxpr/ppermute | solution.py:16
  1021.8 23.8 %collective-permute-start.3 = (f32[6,66,1]{2,1,0:T(8,128)S(1)}, f32[6,66,1]{2,1,0:T(8,128)S(1)}, u32[]{:S(2)}, u32[]{:S(2)}) collective-permute-start(f32[6,66,1]{2,1,0:T(8,128)S(1)} %get-tuple-element.181), channel_id=1, source_target_pairs={{1,0},{2,1},{3,2},{4,3},{5,4},{6,5},{7,6},{9,8},{10,9},{11,10},{12... | collective-permute-start | bytes 4760 | tf_op jit(solution)/shard_map/while/body/eval_jaxpr/ppermute | solution.py:17
  1061.1 24.8 %all-to-all-start = ((f32[64,1,192]{2,1,0:T(1,128)}), f32[64,1,192]{2,1,0:T(1,128)S(1)}, u32[]{:S(2)}, u32[]{:S(2)}) async-start(f32[64,1,192]{2,1,0:T(1,128)} %reshape.136), calls=%async_computation | async-start | bytes 131072 | tf_op jit(solution)/shard_map/while/body/eval_jaxpr/all_to_all | solution.py:42
  1081.3 27.1 %collective-permute-start.2 = (f32[6,66,1]{2,1,0:T(8,128)S(1)}, f32[6,66,1]{2,1,0:T(8,128)S(1)}, u32[]{:S(2)}, u32[]{:S(2)}) collective-permute-start(f32[6,66,1]{2,1,0:T(8,128)S(1)} %get-tuple-element.180), channel_id=1, source_target_pairs={{0,1},{1,2},{2,3},{3,4},{4,5},{5,6},{6,7},{8,9},{9,10},{10,11},{11... | collective-permute-start | bytes 4760 | tf_op jit(solution)/shard_map/while/body/eval_jaxpr/ppermute | solution.py:16
  1084.6 23.8 %collective-permute-start.3 = (f32[6,66,1]{2,1,0:T(8,128)S(1)}, f32[6,66,1]{2,1,0:T(8,128)S(1)}, u32[]{:S(2)}, u32[]{:S(2)}) collective-permute-start(f32[6,66,1]{2,1,0:T(8,128)S(1)} %get-tuple-element.181), channel_id=1, source_target_pairs={{1,0},{2,1},{3,2},{4,3},{5,4},{6,5},{7,6},{9,8},{10,9},{11,10},{12... | collective-permute-start | bytes 4760 | tf_op jit(solution)/shard_map/while/body/eval_jaxpr/ppermute | solution.py:17
  1123.8 24.8 %all-to-all-start = ((f32[64,1,192]{2,1,0:T(1,128)}), f32[64,1,192]{2,1,0:T(1,128)S(1)}, u32[]{:S(2)}, u32[]{:S(2)}) async-start(f32[64,1,192]{2,1,0:T(1,128)} %reshape.136), calls=%async_computation | async-start | bytes 131072 | tf_op jit(solution)/shard_map/while/body/eval_jaxpr/all_to_all | solution.py:42
  1144.1 27.1 %collective-permute-start.2 = (f32[6,66,1]{2,1,0:T(8,128)S(1)}, f32[6,66,1]{2,1,0:T(8,128)S(1)}, u32[]{:S(2)}, u32[]{:S(2)}) collective-permute-start(f32[6,66,1]{2,1,0:T(8,128)S(1)} %get-tuple-element.180), channel_id=1, source_target_pairs={{0,1},{1,2},{2,3},{3,4},{4,5},{5,6},{6,7},{8,9},{9,10},{10,11},{11... | collective-permute-start | bytes 4760 | tf_op jit(solution)/shard_map/while/body/eval_jaxpr/ppermute | solution.py:16
  1147.4 23.8 %collective-permute-start.3 = (f32[6,66,1]{2,1,0:T(8,128)S(1)}, f32[6,66,1]{2,1,0:T(8,128)S(1)}, u32[]{:S(2)}, u32[]{:S(2)}) collective-permute-start(f32[6,66,1]{2,1,0:T(8,128)S(1)} %get-tuple-element.181), channel_id=1, source_target_pairs={{1,0},{2,1},{3,2},{4,3},{5,4},{6,5},{7,6},{9,8},{10,9},{11,10},{12... | collective-permute-start | bytes 4760 | tf_op jit(solution)/shard_map/while/body/eval_jaxpr/ppermute | solution.py:17
  1186.6 24.8 %all-to-all-start = ((f32[64,1,192]{2,1,0:T(1,128)}), f32[64,1,192]{2,1,0:T(1,128)S(1)}, u32[]{:S(2)}, u32[]{:S(2)}) async-start(f32[64,1,192]{2,1,0:T(1,128)} %reshape.136), calls=%async_computation | async-start | bytes 131072 | tf_op jit(solution)/shard_map/while/body/eval_jaxpr/all_to_all | solution.py:42
  1206.8 27.1 %collective-permute-start.2 = (f32[6,66,1]{2,1,0:T(8,128)S(1)}, f32[6,66,1]{2,1,0:T(8,128)S(1)}, u32[]{:S(2)}, u32[]{:S(2)}) collective-permute-start(f32[6,66,1]{2,1,0:T(8,128)S(1)} %get-tuple-element.180), channel_id=1, source_target_pairs={{0,1},{1,2},{2,3},{3,4},{4,5},{5,6},{6,7},{8,9},{9,10},{10,11},{11... | collective-permute-start | bytes 4760 | tf_op jit(solution)/shard_map/while/body/eval_jaxpr/ppermute | solution.py:16
  1210.1 23.8 %collective-permute-start.3 = (f32[6,66,1]{2,1,0:T(8,128)S(1)}, f32[6,66,1]{2,1,0:T(8,128)S(1)}, u32[]{:S(2)}, u32[]{:S(2)}) collective-permute-start(f32[6,66,1]{2,1,0:T(8,128)S(1)} %get-tuple-element.181), channel_id=1, source_target_pairs={{1,0},{2,1},{3,2},{4,3},{5,4},{6,5},{7,6},{9,8},{10,9},{11,10},{12... | collective-permute-start | bytes 4760 | tf_op jit(solution)/shard_map/while/body/eval_jaxpr/ppermute | solution.py:17
  1249.4 24.8 %all-to-all-start = ((f32[64,1,192]{2,1,0:T(1,128)}), f32[64,1,192]{2,1,0:T(1,128)S(1)}, u32[]{:S(2)}, u32[]{:S(2)}) async-start(f32[64,1,192]{2,1,0:T(1,128)} %reshape.136), calls=%async_computation | async-start | bytes 131072 | tf_op jit(solution)/shard_map/while/body/eval_jaxpr/all_to_all | solution.py:42
  1269.6 27.1 %collective-permute-start.2 = (f32[6,66,1]{2,1,0:T(8,128)S(1)}, f32[6,66,1]{2,1,0:T(8,128)S(1)}, u32[]{:S(2)}, u32[]{:S(2)}) collective-permute-start(f32[6,66,1]{2,1,0:T(8,128)S(1)} %get-tuple-element.180), channel_id=1, source_target_pairs={{0,1},{1,2},{2,3},{3,4},{4,5},{5,6},{6,7},{8,9},{9,10},{10,11},{11... | collective-permute-start | bytes 4760 | tf_op jit(solution)/shard_map/while/body/eval_jaxpr/ppermute | solution.py:16
  1272.9 23.8 %collective-permute-start.3 = (f32[6,66,1]{2,1,0:T(8,128)S(1)}, f32[6,66,1]{2,1,0:T(8,128)S(1)}, u32[]{:S(2)}, u32[]{:S(2)}) collective-permute-start(f32[6,66,1]{2,1,0:T(8,128)S(1)} %get-tuple-element.181), channel_id=1, source_target_pairs={{1,0},{2,1},{3,2},{4,3},{5,4},{6,5},{7,6},{9,8},{10,9},{11,10},{12... | collective-permute-start | bytes 4760 | tf_op jit(solution)/shard_map/while/body/eval_jaxpr/ppermute | solution.py:17
  1349.1 7.6 collective-permute-start.8
  (128 other events, 3622.7 us)
Sparse Core Ops, SparseCore 0:
  1299.4 48.8 all-reduce.1
where the time goes:
time: 1380 us; the launch traced here: 1370 us
  starting transfers between devices  502 us (36%)
  local copies, waits for them, and re-layouts  429 us (31%)
  other arithmetic  355 us (26%)
  waiting for transfers between devices  68.2 us (5%)
  between operations  14.9 us (1%)
    scatter-add x20, other arithmetic, mortar(): added = jnp.zeros((6, cells), jnp.float32).at[:, targets].add(got * weights)  304 us
    all_to_all x20, starting transfers between devices, mortar(): lax.all_to_all(sent, ('mx', 'my'), split_axis=1, concat_axis=1, tiled=True)  275 us
    gather x20, local copies, waits for them, and re-layouts, mortar(): sent = field.reshape(6, cells)[:, sources]  177 us
    ppermute x44, starting transfers between devices, extended(): before = lax.ppermute(last, axis, up)  142 us
    reshape x20, local copies, waits for them, and re-layouts, mortar(): return added.reshape(6, rows_x, rows_y)  106 us
    another operation x20, local copies, waits for them, and re-layouts  94.6 us
    ppermute x44, starting transfers between devices, extended(): after = lax.ppermute(first, axis, down)  85.3 us
    psum x1, waiting for transfers between devices, on_device(): total = lax.psum(sens, 'freq')  49 us
  transfers between devices with their start and end apart: 109, of which 24 were waited for; matrix products, arithmetic and copies ran while one was open for 34% of the time, Pallas kernels for 0%

commit v1 on v0

--- a/solution.py
+++ b/solution.py
@@ -1,9 +1,325 @@
+import functools
+
 import jax
 import jax.numpy as jnp
 from jax import lax
+from jax.experimental import pallas as pl
+from jax.experimental.pallas import tpu as pltpu
 from jax.sharding import PartitionSpec as P
 
 ITERS = 20
+MESH = pl.DeviceIdType.MESH
+F32 = jnp.float32
+BF16 = jnp.bfloat16
+
+
+def onehot(a, b):
+    return jnp.where(a == b, 1.0, 0.0).astype(F32)
+
+
+def sweeps_kernel(
+    n_mx,
+    n_my,
+    rhs_ref,
+    dens_ref,
+    stiffness_ref,
+    mass_ref,
+    omega_ref,
+    send_ref,
+    recv_ref,
+    weight_ref,
+    out_ref,
+    field,
+    field_b,
+    stiff_s,
+    gain_p,
+    gain_q,
+    pick_y,
+    pick_x,
+    put_y,
+    put_x,
+    wrow,
+    spread,
+    msg_out,
+    msg_in,
+    y_out,
+    y_in,
+    x_out,
+    x_in,
+    msg_send_sem,
+    msg_recv_sem,
+    own_sem,
+    halo_send_sem,
+    halo_recv_sem,
+):
+    i = lax.axis_index("mx")
+    j = lax.axis_index("my")
+    peers = n_mx * n_my
+    me = i * n_my + j
+    rx, ry = dens_ref.shape
+    slots = send_ref.shape[1]
+    tiles = slots // 128
+
+    def at(di, dj):
+        return {
+            "mx": lax.rem(i + di + n_mx, n_mx),
+            "my": lax.rem(j + dj + n_my, n_my),
+        }
+
+    offsets = [(a, b) for a in range(n_mx) for b in range(n_my) if a or b]
+
+    def far(o):
+        a, b = o
+        return -(min(b, n_my - b) + min(a, n_mx - a) / 2.0)
+
+    offsets.sort(key=far)
+
+    barrier = pltpu.get_barrier_semaphore()
+    for a, b in offsets:
+        pl.semaphore_signal(barrier, inc=1, device_id=at(a, b), device_id_type=MESH)
+
+    w = omega_ref[0]
+    dens = dens_ref[...]
+    mass = mass_ref[...]
+    stiff = dens * dens * dens * stiffness_ref[...]
+    rmass = dens * mass
+    stiff_s[...] = stiff
+
+    lane = lax.broadcasted_iota(jnp.int32, (8, 128), 1)
+    sub = lax.broadcasted_iota(jnp.int32, (8, 128), 0)
+    block = lax.shift_right_logical(lane, 5)
+    comp = lax.bitwise_and(sub, 3)
+    here = block == comp
+
+    sub_y = lax.broadcasted_iota(jnp.int32, (ry, 128), 0)
+    sub_x = lax.broadcasted_iota(jnp.int32, (rx, 128), 0)
+    lane_y = lax.broadcasted_iota(jnp.int32, (128, ry), 1)
+    lane_row = lax.broadcasted_iota(jnp.int32, (1, 128), 1)
+    low = lane_row < rx
+    for t in range(tiles + 1):
+        cols = slice(t * 128, (t + 1) * 128)
+        if t < tiles:
+            src = send_ref[:, cols]
+            dst = recv_ref[:, cols]
+            sx, sy = lax.shift_right_logical(src, 8), lax.bitwise_and(src, ry - 1)
+            dx, dy = lax.shift_right_logical(dst, 8), lax.bitwise_and(dst, ry - 1)
+        else:
+            sx = dx = jnp.where(low, lane_row, lane_row - rx)
+            sy = jnp.where(low, 0, ry - 1)
+            dy = jnp.where(low, ry - 1, 0)
+        pick_y[:, cols] = onehot(sub_y, sy).astype(BF16)
+        pick_x[:, cols] = onehot(sub_x, sx)
+        put_x[:, cols] = onehot(sub_x, dx).astype(BF16)
+        turned = jnp.broadcast_to(dy.astype(F32), (128, 128)).T.astype(jnp.int32)
+        put_y[cols, :] = onehot(lane_y, jnp.concatenate([turned] * (ry // 128), axis=1)).astype(BF16)
+    wrow[:, :slots] = weight_ref[...]
+    eye_low = onehot(sub_x, lane_row)
+    eye_high = onehot(sub_x, lane_row - rx)
+    wrow[:, slots:] = jnp.sum(
+        stiff[:, ry - 1 :] * eye_low + stiff[:, :1] * eye_high, axis=0, keepdims=True
+    )
+
+    whole = weight_ref[...]
+    hi = whole.astype(BF16)
+    rest = whole - hi.astype(F32)
+    mid = rest.astype(BF16)
+    lo = (rest - mid.astype(F32)).astype(BF16)
+    mdiag = jnp.zeros((rx, ry), F32)
+    for piece in (hi, mid, lo):
+        spread[0:rx, :slots] = put_x[:, :slots] * jnp.broadcast_to(piece, (rx, slots))
+        mdiag += jnp.dot(spread[0:rx, :slots], put_y[:slots, :], preferred_element_type=F32)
+
+    real_d = 4.4 * stiff + 0.3 + mdiag - w * w * rmass
+    imag_d = 0.2 * w * (stiff + rmass)
+    den = real_d * real_d + imag_d * imag_d
+    gain_p[...] = real_d / den
+    gain_q[...] = imag_d / den
+
+    def update(h):
+        p, q = gain_p[...], gain_q[...]
+        for c in range(3):
+            re, im = h(c), h(c + 3)
+            new_re = re * p + im * q
+            new_im = im * p - re * q
+            for k, v in ((c, new_re), (c + 3, new_im)):
+                field[k, :, :] = v
+                field_b[k * rx : (k + 1) * rx, :] = v.astype(BF16)
+
+    update(lambda c: rhs_ref[c])
+
+    pl.semaphore_wait(barrier, peers - 1)
+
+    up_ok = jnp.where(i > 0, 1.0, 0.0).astype(F32)
+    down_ok = jnp.where(i < n_mx - 1, 1.0, 0.0).astype(F32)
+    left_ok = jnp.where(j > 0, 1.0, 0.0).astype(F32)
+    right_ok = jnp.where(j < n_my - 1, 1.0, 0.0).astype(F32)
+    zero_row = jnp.zeros((1, 128), F32)
+
+    def pick(cols, width):
+        g = jnp.dot(field_b[...], pick_y[:, cols], preferred_element_type=F32)
+        mask = pick_x[:, cols]
+        rows = [
+            jnp.sum(g[c * rx : (c + 1) * rx] * mask, axis=0, keepdims=True) for c in range(6)
+        ]
+        zero = jnp.zeros((1, width), F32)
+        return jnp.concatenate(rows[:3] + [zero] + rows[3:] + [zero], axis=0)
+
+    def remote(src, dst, ssem, rsem, to):
+        return pltpu.make_async_remote_copy(
+            src_ref=src, dst_ref=dst, send_sem=ssem, recv_sem=rsem, device_id=to, device_id_type=MESH
+        )
+
+    def sweep(step, carry):
+        par = lax.rem(step, 2)
+
+        for c in range(6):
+            x_out[0, c : c + 1, :] = field[c, 0:1, :]
+            x_out[1, c : c + 1, :] = field[c, rx - 1 : rx, :]
+        halo = halo_recv_sem.at[par]
+        remote(x_out.at[0], x_in.at[par, 1], halo_send_sem.at[0], halo.at[1], at(-1, 0)).start()
+        remote(x_out.at[1], x_in.at[par, 0], halo_send_sem.at[1], halo.at[0], at(1, 0)).start()
+
+        for t in range(tiles // 2):
+            rows = pick(slice(t * 256, (t + 1) * 256), 256)
+            for half in range(2):
+                r = rows[:, half * 128 : (half + 1) * 128]
+                x = jnp.where(
+                    comp == 1, pltpu.roll(r, 32, 1), jnp.where(comp == 2, pltpu.roll(r, 64, 1), r)
+                )
+                for d in range(4):
+                    y = x if d == 0 else pltpu.roll(x, 128 - 32 * d, 1)
+                    z = jnp.where(here, y, 0.0)
+                    m = jnp.concatenate(
+                        [
+                            jnp.sum(z[:4], axis=0, keepdims=True),
+                            jnp.sum(z[4:], axis=0, keepdims=True),
+                        ],
+                        axis=0,
+                    )
+                    msg_out[(2 * t + half) * 4 + d] = m.astype(BF16)
+        own = pltpu.make_async_copy(msg_out.at[me], msg_in.at[par, me], own_sem)
+        own.start()
+        for a, b in offsets:
+            to = at(a, b)
+            remote(
+                msg_out.at[to["mx"] * n_my + to["my"]],
+                msg_in.at[par, me],
+                msg_send_sem,
+                msg_recv_sem.at[par],
+                to,
+            ).start()
+
+        y_out[...] = pick(slice(slots, slots + 128), 128)
+        remote(y_out, y_in.at[par, 1], halo_send_sem.at[2], halo.at[3], at(0, -1)).start()
+        remote(y_out, y_in.at[par, 0], halo_send_sem.at[3], halo.at[2], at(0, 1)).start()
+
+        for side in range(2):
+            pltpu.make_async_copy(x_in.at[par, side], x_in.at[par, side], halo.at[side]).wait()
+            pltpu.make_async_copy(y_in.at[par, side], y_in.at[par, side], halo.at[2 + side]).wait()
+        own.wait()
+        most = pl.ds(0, peers - 1)
+        pltpu.make_async_copy(
+            msg_in.at[par, most], msg_in.at[par, most], msg_recv_sem.at[par]
+        ).wait()
+
+        for t in range(tiles + 1):
+            cols = slice(t * 128, (t + 1) * 128)
+            if t < tiles:
+                got = None
+                for d in range(4):
+                    m = msg_in[par, 4 * t + d].astype(F32)
+                    u = jnp.concatenate(
+                        [
+                            jnp.broadcast_to(m[0:1], (4, 128)),
+                            jnp.broadcast_to(m[1:2], (4, 128)),
+                        ],
+                        axis=0,
+                    )
+                    u = jnp.where(here, u, 0.0)
+                    if d:
+                        u = pltpu.roll(u, 32 * d, 1)
+                    got = u if got is None else got + u
+                got = jnp.where(
+                    comp == 1,
+                    pltpu.roll(got, 96, 1),
+                    jnp.where(comp == 2, pltpu.roll(got, 64, 1), got),
+                )
+            else:
+                got = jnp.where(
+                    lane < rx, y_in[par, 1] * right_ok, y_in[par, 0] * left_ok
+                )
+            got = got * wrow[:, cols]
+            mask = put_x[:, cols]
+            for c in range(6):
+                r = c + c // 3
+                spread[c * rx : (c + 1) * rx, cols] = mask * jnp.broadcast_to(
+                    got[r : r + 1].astype(BF16), (rx, 128)
+                )
+        coupled = jnp.dot(spread[...], put_y[...], preferred_element_type=F32)
+
+        pltpu.make_async_copy(msg_out.at[most], msg_out.at[most], msg_send_sem).wait()
+        for side in range(2):
+            pltpu.make_async_copy(x_out.at[side], x_out.at[side], halo_send_sem.at[side]).wait()
+            pltpu.make_async_copy(y_out, y_out, halo_send_sem.at[2 + side]).wait()
+
+        st = stiff_s[...]
+        lane_w = lax.broadcasted_iota(jnp.int32, (rx, ry), 1)
+        sub_w = lax.broadcasted_iota(jnp.int32, (rx, ry), 0)
+
+        def h(c):
+            f = field[c]
+            above = jnp.broadcast_to(x_in[par, 0, c : c + 1, :] * up_ok, (rx, ry))
+            below = jnp.broadcast_to(x_in[par, 1, c : c + 1, :] * down_ok, (rx, ry))
+            nb = jnp.where(sub_w == 0, above, pltpu.roll(f, 1, 0))
+            nb += jnp.where(sub_w == rx - 1, below, pltpu.roll(f, rx - 1, 0))
+            nb += jnp.where(lane_w == 0, 0.0, pltpu.roll(f, 1, 1))
+            nb += jnp.where(lane_w == ry - 1, 0.0, pltpu.roll(f, ry - 1, 1))
+            return rhs_ref[c] + st * nb + coupled[c * rx : (c + 1) * rx]
+
+        update(h)
+        return carry
+
+    lax.fori_loop(1, ITERS, sweep, 0)
+    out_ref[...] = field[...]
+
+
+def solve(n_mx, n_my, rhs, density, stiffness, mass, omega, send_rows, recv_rows, mortar_weight):
+    rx, ry = density.shape
+    slots = send_rows.shape[1]
+    wide = slots + 128
+    peers = n_mx * n_my
+    vmem = pl.BlockSpec(memory_space=pltpu.VMEM)
+    return pl.pallas_call(
+        functools.partial(sweeps_kernel, n_mx, n_my),
+        out_shape=jax.ShapeDtypeStruct((6, rx, ry), F32),
+        in_specs=[vmem] * 4 + [pl.BlockSpec(memory_space=pltpu.SMEM)] + [vmem] * 3,
+        out_specs=vmem,
+        scratch_shapes=[
+            pltpu.VMEM((6, rx, ry), F32),
+            pltpu.VMEM((6 * rx, ry), BF16),
+            pltpu.VMEM((rx, ry), F32),
+            pltpu.VMEM((rx, ry), F32),
+            pltpu.VMEM((rx, ry), F32),
+            pltpu.VMEM((ry, wide), BF16),
+            pltpu.VMEM((rx, wide), F32),
+            pltpu.VMEM((wide, ry), BF16),
+            pltpu.VMEM((rx, wide), BF16),
+            pltpu.VMEM((1, wide), F32),
+            pltpu.VMEM((6 * rx, wide), BF16),
+            pltpu.VMEM((peers, 2, 128), BF16),
+            pltpu.VMEM((2, peers, 2, 128), BF16),
+            pltpu.VMEM((8, 128), F32),
+            pltpu.VMEM((2, 2, 8, 128), F32),
+            pltpu.VMEM((2, 8, ry), F32),
+            pltpu.VMEM((2, 2, 8, ry), F32),
+            pltpu.SemaphoreType.DMA,
+            pltpu.SemaphoreType.DMA((2,)),
+            pltpu.SemaphoreType.DMA,
+            pltpu.SemaphoreType.DMA((4,)),
+            pltpu.SemaphoreType.DMA((2, 4)),
+        ],
+        compiler_params=pltpu.CompilerParams(collective_id=0, has_side_effects=True),
+    )(rhs, density, stiffness, mass, omega, send_rows, recv_rows, mortar_weight)
 
 
 def extended(x, sides, width):
@@ -23,37 +339,13 @@
     adjoint_rhs, state, density, stiffness, mass, omega, send_rows, recv_rows, mortar_weight
 ):
     rows_x, rows_y = density.shape
-    cells = rows_x * rows_y
     w = omega[0]
-    stiff = density**3 * stiffness
     dstiff = 3.0 * density**2 * stiffness
-    rmass = density * mass
-    sources = send_rows[0]
-    targets = recv_rows[0]
-    weights = mortar_weight[0]
-    mdiag = jnp.zeros((cells,), jnp.float32).at[targets].add(weights).reshape(rows_x, rows_y)
-    real_d = 4.4 * stiff + 0.3 + mdiag - w * w * rmass
-    imag_d = 0.2 * w * (stiff + rmass)
-    den = real_d * real_d + imag_d * imag_d
     rhs = adjoint_rhs.reshape(6, rows_x, rows_y)
-
-    def mortar(field):
-        sent = field.reshape(6, cells)[:, sources]
-        got = lax.all_to_all(sent, ("mx", "my"), split_axis=1, concat_axis=1, tiled=True)
-        added = jnp.zeros((6, cells), jnp.float32).at[:, targets].add(got * weights)
-        return added.reshape(6, rows_x, rows_y)
-
-    def sweep(step, field):
-        padded = extended(field, (("mx", 1), ("my", 2)), 1)
-        beside = (
-            padded[:, 2:, 1:-1] + padded[:, :-2, 1:-1] + padded[:, 1:-1, 2:] + padded[:, 1:-1, :-2]
-        )
-        h = rhs + stiff * beside + mortar(field)
-        new_re = (h[:3] * real_d + h[3:] * imag_d) / den
-        new_im = (h[3:] * real_d - h[:3] * imag_d) / den
-        return jnp.concatenate([new_re, new_im], axis=0)
-
-    field = lax.fori_loop(0, ITERS, sweep, jnp.zeros((6, rows_x, rows_y), jnp.float32))
+    field = solve(
+        lax.axis_size("mx"), lax.axis_size("my"),
+        rhs, density, stiffness, mass, omega, send_rows, recv_rows, mortar_weight,
+    )
     state_six = state.reshape(6, rows_x, rows_y)
     state_pad = extended(state_six, (("mx", 1), ("my", 2)), 1).astype(jnp.float32)
     u = state_six.astype(jnp.float32)

time: 1380 us -> 265 us (0.19)
  starting transfers between devices: 502 us -> 24.3 us
  local copies, waits for them, and re-layouts: 429 us -> 2.34 us
  other arithmetic: 355 us -> 4.13 us
  Pallas kernels: 0 us -> 170 us
  waiting for transfers between devices: 68.2 us -> 47.3 us
    scatter-add x21 -> x0, other arithmetic: 316 us -> none  [the longest x20 304 us: mortar(): added = jnp.zeros((6, cells), jnp.float32).at[:, targets].add(got * weights)]
    all_to_all x20 -> x0, starting transfers between devices: 275 us -> none  [mortar(): lax.all_to_all(sent, ('mx', 'my'), split_axis=1, concat_axis=1, tiled=True)]
    gather x20 -> x0, local copies, waits for them, and re-layouts: 177 us -> none  [mortar(): sent = field.reshape(6, cells)[:, sources]]
    pallas_call x0 -> x1, Pallas kernels: none -> 170 us  [solve(): pl.pallas_call(functools.partial(sweeps_kernel, n_mx, n_my), out_shape=ja...]
    ppermute x44 -> x4, starting transfers between devices: 142 us -> 15 us  [extended(): before = lax.ppermute(last, axis, up)]
    reshape x21 -> x0, local copies, waits for them, and re-layouts: 106 us -> none  [the longest x20 106 us: mortar(): return added.reshape(6, rows_x, rows_y)]
    another operation x20 -> x0, local copies, waits for them, and re-layouts: 94.6 us -> none
    ppermute x44 -> x4, starting transfers between devices: 85.3 us -> 9.22 us  [extended(): after = lax.ppermute(first, axis, down)]
  transfers between devices with their start and end apart: 109 -> 9, of which waited for: 24 -> 5; matrix products, arithmetic and copies ran while one was open for 34% -> 0% of each run, Pallas kernels for 0% -> 65%
where the time goes in v1:
time: 265 us; the launch traced here: 263 us
  Pallas kernels  170 us (64%)
  waiting for transfers between devices  47.3 us (18%)
  starting transfers between devices  24.3 us (9%)
  between operations  14.9 us (6%)
  other arithmetic  4.13 us (2%)
    pallas_call x1, Pallas kernels, solve(): pl.pallas_call(functools.partial(sweeps_kernel, n_mx, n_my), out_shape=ja...  170 us
    psum x1, waiting for transfers between devices, on_device(): total = lax.psum(sens, 'freq')  44.2 us
    ppermute x4, starting transfers between devices, extended(): before = lax.ppermute(last, axis, up)  15 us
    ppermute x4, starting transfers between devices, extended(): after = lax.ppermute(first, axis, down)  9.22 us
  transfers between devices with their start and end apart: 9, of which 5 were waited for; matrix products, arithmetic and copies ran while one was open for 0% of the time, Pallas kernels for 65%

profile of v1, /device:TPU:1, one launch (start us, length us, event | category | flops | bytes accessed | tf_op | source)
XLA Modules:
  0.0 262.9 jit_solution(25346962866478902)
XLA Ops:
  7.2 0.0 all-reduce.2.cloned.1.call-start
  7.2 0.8 fusion.13
  8.0 4.5 %collective-permute-start = (bf16[6,1,256]{2,1,0:T(2,128)(2,1)S(1)}, bf16[6,1,256]{2,1,0:T(2,128)(2,1)S(1)}, u32[]{:S(2)}, u32[]{:S(2)}) collective-permute-start(bf16[6,1,256]{2,1,0:T(2,128)(2,1)S(1)} %get-tuple-element.6), channel_id=1, source_target_pairs={{0,8},{8,16},{16,24},{24,32},{32,40},{40,48},{48,56},{1,9},{9,17},... | collective-permute-start | bytes 9224 | tf_op jit(solution)/shard_map/ppermute | solution.py:332
  12.5 0.0 copy-start.2
  12.5 0.0 copy-start.4
  12.5 0.0 copy-start.5
  12.5 2.1 collective-permute-start.1
  14.6 1.0 bitcast_convert_fusion
  15.5 0.0 copy-start.1
  16.2 0.0 copy-done.2
  16.3 0.0 copy-done.4
  16.3 0.0 copy-done.5
  16.3 0.0 collective-permute-done
  16.3 1.3 collective-permute-done.1
  17.6 0.0 copy-done.1
  17.6 0.1 pad_maximum_fusion
  17.7 0.1 fusion.12
  17.8 3.5 %collective-permute-start.2 = (bf16[6,66,1]{2,1,0:T(8,128)(2,1)S(1)}, bf16[6,66,1]{2,1,0:T(8,128)(2,1)S(1)}, u32[]{:S(2)}, u32[]{:S(2)}) collective-permute-start(bf16[6,66,1]{2,1,0:T(8,128)(2,1)S(1)} %get-tuple-element.4), channel_id=1, source_target_pairs={{0,1},{1,2},{2,3},{3,4},{4,5},{5,6},{6,7},{8,9},{9,10},{10,11},{11... | collective-permute-start | bytes 2384 | tf_op jit(solution)/shard_map/ppermute | solution.py:332
  21.3 1.3 collective-permute-start.3
  22.7 170.0 %shard_map.104 = f32[6,64,256]{2,1,0:T(8,128)} custom-call(f32[6,64,256]{2,1,0:T(8,128)} %bitcast.10, f32[64,256]{1,0:T(8,128)} %dens_ref.1, f32[64,256]{1,0:T(8,128)} %stiffness_ref.1, f32[64,256]{1,0:T(8,128)} %mass_ref.1, f32[1]{0:T(128)S(6)} %copy.13.omega_ref, s32[1,2048]{1,0:T(1,128)} %send_ref.1, s32[1,2048]{1,0:T(1,128)} %recv_ref.1, ...), custom_call_target="tpu_custom_call" | custom-call | tf_op jit(solution)/shard_map/pallas_call | solution.py:292
  192.6 0.0 collective-permute-done.2
  192.6 0.0 collective-permute-done.3
  192.6 0.3 maximum_convert_fusion
  192.9 0.0 copy-start
  192.9 0.4 slice_add_fusion
  193.3 0.6 copy-done
  193.9 0.1 fusion.3
  194.0 0.6 neg.3
  194.6 0.0 copy-start.3
  194.6 0.0 all-reduce.2.cloned.1.call-update
  194.7 44.2 %all-reduce.2.cloned.1.call-done = f32[64,256]{1,0:T(8,128)} async-done(((f32[64,256]{1,0:T(8,128)}), f32[64,256]{1,0:T(8,128)}) %all-reduce.2.cloned.1.call-update) | async-done | bytes 65552 | tf_op jit(solution)/shard_map/psum | solution.py:363
  238.9 0.0 copy-done.3
  238.9 0.8 mul.124
  239.8 4.6 %collective-permute-start.4 = (f32[1,256]{1,0:T(1,128)S(1)}, f32[1,256]{1,0:T(1,128)S(1)}, u32[]{:S(2)}, u32[]{:S(2)}) collective-permute-start(f32[1,256]{1,0:T(1,128)S(1)} %get-tuple-element.13), channel_id=1, source_target_pairs={{8,0},{16,8},{24,16},{32,24},{40,32},{48,40},{56,48},{9,1},{17,9},... | collective-permute-start | bytes 3080 | tf_op jit(solution)/shard_map/ppermute | solution.py:333
  244.4 3.0 %collective-permute-start.5 = (f32[1,256]{1,0:T(1,128)S(1)}, f32[1,256]{1,0:T(1,128)S(1)}, u32[]{:S(2)}, u32[]{:S(2)}) collective-permute-start(f32[1,256]{1,0:T(1,128)S(1)} %get-tuple-element.12), channel_id=1, source_target_pairs={{0,8},{8,16},{16,24},{24,32},{32,40},{40,48},{48,56},{1,9},{9,17},... | collective-permute-start | bytes 3080 | tf_op jit(solution)/shard_map/ppermute | solution.py:332
  247.4 0.0 collective-permute-done.4
  247.4 0.7 collective-permute-done.5
  248.1 0.1 fusion.14
  248.2 1.3 collective-permute-start.6
  249.5 4.0 %collective-permute-start.7 = (f32[66,1]{1,0:T(8,128)S(1)}, f32[66,1]{1,0:T(8,128)S(1)}, u32[]{:S(2)}, u32[]{:S(2)}) collective-permute-start(f32[66,1]{1,0:T(8,128)S(1)} %get-tuple-element.8), channel_id=1, source_target_pairs={{0,1},{1,2},{2,3},{3,4},{4,5},{5,6},{6,7},{8,9},{9,10},{10,11},{11... | collective-permute-start | bytes 800 | tf_op jit(solution)/shard_map/ppermute | solution.py:332
  253.5 0.1 collective-permute-done.6
  253.5 1.0 collective-permute-done.7
  254.5 0.1 maximum_maximum_fusion
  254.6 0.8 fusion.8
  255.4 0.7 copy.14
  (4 shorter events, 0.1 us)
Async XLA Ops:
  7.2 231.7 %all-reduce.2.cloned.1.call-start = ((), (), s32[]{:S(2)}) async-start(), calls=%async_computation | async-start | bytes 131072 | tf_op jit(solution)/shard_map/psum | solution.py:363
  8.0 8.3 %collective-permute-start = (bf16[6,1,256]{2,1,0:T(2,128)(2,1)S(1)}, bf16[6,1,256]{2,1,0:T(2,128)(2,1)S(1)}, u32[]{:S(2)}, u32[]{:S(2)}) collective-permute-start(bf16[6,1,256]{2,1,0:T(2,128)(2,1)S(1)} %get-tuple-element.6), channel_id=1, source_target_pairs={{0,8},{8,16},{16,24},{24,32},{32,40},{40,48},{48,56},{1,9},{9,17},... | collective-permute-start | bytes 9224 | tf_op jit(solution)/shard_map/ppermute | solution.py:332
  12.5 3.8 %copy-start.2 = (f32[64,256]{1,0:T(8,128)S(1)}, f32[64,256]{1,0:T(8,128)}, u32[]{:S(2)}) copy-start(f32[64,256]{1,0:T(8,128)} %dens_ref.1) | copy-start | bytes 196612
  12.5 3.8 %copy-start.4 = (f32[64,256]{1,0:T(8,128)S(1)}, f32[64,256]{1,0:T(8,128)}, u32[]{:S(2)}) copy-start(f32[64,256]{1,0:T(8,128)} %mass_ref.1) | copy-start | bytes 196612
  12.5 3.8 %copy-start.5 = (f32[64,256]{1,0:T(8,128)S(1)}, f32[64,256]{1,0:T(8,128)}, u32[]{:S(2)}) copy-start(f32[64,256]{1,0:T(8,128)} %stiffness_ref.1) | copy-start | bytes 196612
  12.5 5.1 %collective-permute-start.1 = (bf16[6,1,256]{2,1,0:T(2,128)(2,1)S(1)}, bf16[6,1,256]{2,1,0:T(2,128)(2,1)S(1)}, u32[]{:S(2)}, u32[]{:S(2)}) collective-permute-start(bf16[6,1,256]{2,1,0:T(2,128)(2,1)S(1)} %get-tuple-element.7), channel_id=1, source_target_pairs={{8,0},{16,8},{24,16},{32,24},{40,32},{48,40},{56,48},{9,1},{17,9},... | collective-permute-start | bytes 9224 | tf_op jit(solution)/shard_map/ppermute | solution.py:333
  15.5 2.1 copy-start.1
  17.8 174.8 %collective-permute-start.2 = (bf16[6,66,1]{2,1,0:T(8,128)(2,1)S(1)}, bf16[6,66,1]{2,1,0:T(8,128)(2,1)S(1)}, u32[]{:S(2)}, u32[]{:S(2)}) collective-permute-start(bf16[6,66,1]{2,1,0:T(8,128)(2,1)S(1)} %get-tuple-element.4), channel_id=1, source_target_pairs={{0,1},{1,2},{2,3},{3,4},{4,5},{5,6},{6,7},{8,9},{9,10},{10,11},{11... | collective-permute-start | bytes 2384 | tf_op jit(solution)/shard_map/ppermute | solution.py:332
  21.3 171.3 %collective-permute-start.3 = (bf16[6,66,1]{2,1,0:T(8,128)(2,1)S(1)}, bf16[6,66,1]{2,1,0:T(8,128)(2,1)S(1)}, u32[]{:S(2)}, u32[]{:S(2)}) collective-permute-start(bf16[6,66,1]{2,1,0:T(8,128)(2,1)S(1)} %get-tuple-element.5), channel_id=1, source_target_pairs={{1,0},{2,1},{3,2},{4,3},{5,4},{6,5},{7,6},{9,8},{10,9},{11,10},{12... | collective-permute-start | bytes 2384 | tf_op jit(solution)/shard_map/ppermute | solution.py:333
  192.9 1.0 copy-start
  194.6 44.3 %copy-start.3 = (f32[64,256]{1,0:T(8,128)S(1)}, f32[64,256]{1,0:T(8,128)}, u32[]{:S(2)}) copy-start(f32[64,256]{1,0:T(8,128)} %dens_ref.1) | copy-start | bytes 196612
  239.8 7.6 %collective-permute-start.4 = (f32[1,256]{1,0:T(1,128)S(1)}, f32[1,256]{1,0:T(1,128)S(1)}, u32[]{:S(2)}, u32[]{:S(2)}) collective-permute-start(f32[1,256]{1,0:T(1,128)S(1)} %get-tuple-element.13), channel_id=1, source_target_pairs={{8,0},{16,8},{24,16},{32,24},{40,32},{48,40},{56,48},{9,1},{17,9},... | collective-permute-start | bytes 3080 | tf_op jit(solution)/shard_map/ppermute | solution.py:333
  244.4 3.7 %collective-permute-start.5 = (f32[1,256]{1,0:T(1,128)S(1)}, f32[1,256]{1,0:T(1,128)S(1)}, u32[]{:S(2)}, u32[]{:S(2)}) collective-permute-start(f32[1,256]{1,0:T(1,128)S(1)} %get-tuple-element.12), channel_id=1, source_target_pairs={{0,8},{8,16},{16,24},{24,32},{32,40},{40,48},{48,56},{1,9},{9,17},... | collective-permute-start | bytes 3080 | tf_op jit(solution)/shard_map/ppermute | solution.py:332
  248.2 5.3 %collective-permute-start.6 = (f32[66,1]{1,0:T(8,128)S(1)}, f32[66,1]{1,0:T(8,128)S(1)}, u32[]{:S(2)}, u32[]{:S(2)}) collective-permute-start(f32[66,1]{1,0:T(8,128)S(1)} %get-tuple-element.9), channel_id=1, source_target_pairs={{1,0},{2,1},{3,2},{4,3},{5,4},{6,5},{7,6},{9,8},{10,9},{11,10},{12... | collective-permute-start | bytes 800 | tf_op jit(solution)/shard_map/ppermute | solution.py:333
  249.5 5.0 %collective-permute-start.7 = (f32[66,1]{1,0:T(8,128)S(1)}, f32[66,1]{1,0:T(8,128)S(1)}, u32[]{:S(2)}, u32[]{:S(2)}) collective-permute-start(f32[66,1]{1,0:T(8,128)S(1)} %get-tuple-element.8), channel_id=1, source_target_pairs={{0,1},{1,2},{2,3},{3,4},{4,5},{5,6},{6,7},{8,9},{9,10},{10,11},{11... | collective-permute-start | bytes 800 | tf_op jit(solution)/shard_map/ppermute | solution.py:332
Sparse Core Ops, SparseCore 0:
  194.8 44.0 all-reduce.1

commit v2 on v1

--- a/solution.py
+++ b/solution.py
@@ -18,9 +18,11 @@
 
 
 def sweeps_kernel(
+    n_freq,
     n_mx,
     n_my,
     rhs_ref,
+    state_ref,
     dens_ref,
     stiffness_ref,
     mass_ref,
@@ -29,8 +31,10 @@
     recv_ref,
     weight_ref,
     out_ref,
+    filt_ref,
     field,
     field_b,
+    field_l,
     stiff_s,
     gain_p,
     gain_q,
@@ -51,7 +55,23 @@
     own_sem,
     halo_send_sem,
     halo_recv_sem,
+    tangent,
+    sx_out,
+    sx_in,
+    sy_out,
+    sy_in,
+    state_send_sem,
+    state_recv_sem,
+    sens_out,
+    sens_in,
+    edge_out,
+    edge_in,
+    sens_send_sem,
+    sens_recv_sem,
+    edge_send_sem,
+    edge_recv_sem,
 ):
+    fr = lax.axis_index("freq")
     i = lax.axis_index("mx")
     j = lax.axis_index("my")
     peers = n_mx * n_my
@@ -60,8 +80,9 @@
     slots = send_ref.shape[1]
     tiles = slots // 128
 
-    def at(di, dj):
+    def at(di, dj, df=0):
         return {
+            "freq": lax.rem(fr + df, n_freq),
             "mx": lax.rem(i + di + n_mx, n_mx),
             "my": lax.rem(j + dj + n_my, n_my),
         }
@@ -77,6 +98,10 @@
     barrier = pltpu.get_barrier_semaphore()
     for a, b in offsets:
         pl.semaphore_signal(barrier, inc=1, device_id=at(a, b), device_id_type=MESH)
+    around = [(a, b) for a in (-1, 0, 1) for b in (-1, 0, 1)]
+    for df in range(1, n_freq):
+        for a, b in around:
+            pl.semaphore_signal(barrier, inc=1, device_id=at(a, b, df), device_id_type=MESH)
 
     w = omega_ref[0]
     dens = dens_ref[...]
@@ -112,6 +137,7 @@
         put_x[:, cols] = onehot(sub_x, dx).astype(BF16)
         turned = jnp.broadcast_to(dy.astype(F32), (128, 128)).T.astype(jnp.int32)
         put_y[cols, :] = onehot(lane_y, jnp.concatenate([turned] * (ry // 128), axis=1)).astype(BF16)
+    put_y[slots + 128 :, :] = put_y[slots : slots + 128, :]
     wrow[:, :slots] = weight_ref[...]
     eye_low = onehot(sub_x, lane_row)
     eye_high = onehot(sub_x, lane_row - rx)
@@ -143,11 +169,13 @@
             new_im = im * p - re * q
             for k, v in ((c, new_re), (c + 3, new_im)):
                 field[k, :, :] = v
-                field_b[k * rx : (k + 1) * rx, :] = v.astype(BF16)
+                high = v.astype(BF16)
+                field_b[k * rx : (k + 1) * rx, :] = high
+                field_l[k * rx : (k + 1) * rx, :] = (v - high.astype(F32)).astype(BF16)
 
     update(lambda c: rhs_ref[c])
 
-    pl.semaphore_wait(barrier, peers - 1)
+    pl.semaphore_wait(barrier, peers - 1 + 9 * (n_freq - 1))
 
     up_ok = jnp.where(i > 0, 1.0, 0.0).astype(F32)
     down_ok = jnp.where(i < n_mx - 1, 1.0, 0.0).astype(F32)
@@ -155,8 +183,8 @@
     right_ok = jnp.where(j < n_my - 1, 1.0, 0.0).astype(F32)
     zero_row = jnp.zeros((1, 128), F32)
 
-    def pick(cols, width):
-        g = jnp.dot(field_b[...], pick_y[:, cols], preferred_element_type=F32)
+    def pick(cols, width, source):
+        g = jnp.dot(source, pick_y[:, cols], preferred_element_type=F32)
         mask = pick_x[:, cols]
         rows = [
             jnp.sum(g[c * rx : (c + 1) * rx] * mask, axis=0, keepdims=True) for c in range(6)
@@ -169,6 +197,65 @@
             src_ref=src, dst_ref=dst, send_sem=ssem, recv_sem=rsem, device_id=to, device_id_type=MESH
         )
 
+    edge_cols = slice(slots, slots + 128)
+
+    def scatter(got, start, mask):
+        for c in range(6):
+            r = c + c // 3
+            spread[c * rx : (c + 1) * rx, start : start + 128] = mask * jnp.broadcast_to(
+                got[r : r + 1].astype(BF16), (rx, 128)
+            )
+
+    lane_w = lax.broadcasted_iota(jnp.int32, (rx, ry), 1)
+    sub_w = lax.broadcasted_iota(jnp.int32, (rx, ry), 0)
+
+    def across_x(f, above, below):
+        up = jnp.where(sub_w == 0, jnp.broadcast_to(above, (rx, ry)), pltpu.roll(f, 1, 0))
+        down = jnp.where(
+            sub_w == rx - 1, jnp.broadcast_to(below, (rx, ry)), pltpu.roll(f, rx - 1, 0)
+        )
+        return up + down
+
+    def across_y(f, before, after):
+        left = jnp.where(lane_w == 0, before, pltpu.roll(f, 1, 1))
+        return left + jnp.where(lane_w == ry - 1, after, pltpu.roll(f, ry - 1, 1))
+
+    for c in range(6):
+        sx_out[0, c : c + 1, :] = state_ref[c, 0:1, :].astype(F32)
+        sx_out[1, c : c + 1, :] = state_ref[c, rx - 1 : rx, :].astype(F32)
+    sy_out[...] = pick(edge_cols, 128, state_ref[...].reshape(6 * rx, ry))
+    state_copies = [
+        remote(sx_out.at[0], sx_in.at[1], state_send_sem.at[0], state_recv_sem.at[1], at(-1, 0)),
+        remote(sx_out.at[1], sx_in.at[0], state_send_sem.at[1], state_recv_sem.at[0], at(1, 0)),
+        remote(sy_out, sy_in.at[1], state_send_sem.at[2], state_recv_sem.at[3], at(0, -1)),
+        remote(sy_out, sy_in.at[0], state_send_sem.at[3], state_recv_sem.at[2], at(0, 1)),
+    ]
+    for copy in state_copies:
+        copy.start()
+
+    def tangents():
+        for copy in state_copies:
+            copy.wait()
+        got = jnp.where(lane < rx, sy_in[1] * right_ok, sy_in[0] * left_ok)
+        scatter(got, slots, put_x[:, edge_cols])
+        sides = jnp.dot(spread[:, edge_cols], put_y[edge_cols, :], preferred_element_type=F32)
+        d = dens_ref[...]
+        dstiff = 3.0 * (d * d) * stiffness_ref[...]
+        m = mass_ref[...]
+        da = 4.4 * dstiff - w * w * m
+        db = 0.2 * w * (dstiff + m)
+
+        def beside(c):
+            u = state_ref[c].astype(F32)
+            nb = across_x(u, sx_in[0, c : c + 1, :] * up_ok, sx_in[1, c : c + 1, :] * down_ok)
+            return u, nb + across_y(u, 0.0, 0.0) + sides[c * rx : (c + 1) * rx]
+
+        for c in range(3):
+            u_re, nb_re = beside(c)
+            u_im, nb_im = beside(c + 3)
+            tangent[c, :, :] = da * u_re - db * u_im - dstiff * nb_re
+            tangent[c + 3, :, :] = da * u_im + db * u_re - dstiff * nb_im
+
     def sweep(step, carry):
         par = lax.rem(step, 2)
 
@@ -180,7 +267,7 @@
         remote(x_out.at[1], x_in.at[par, 0], halo_send_sem.at[1], halo.at[0], at(1, 0)).start()
 
         for t in range(tiles // 2):
-            rows = pick(slice(t * 256, (t + 1) * 256), 256)
+            rows = pick(slice(t * 256, (t + 1) * 256), 256, field_b[...])
             for half in range(2):
                 r = rows[:, half * 128 : (half + 1) * 128]
                 x = jnp.where(
@@ -209,9 +296,11 @@
                 to,
             ).start()
 
-        y_out[...] = pick(slice(slots, slots + 128), 128)
+        y_out[...] = pick(edge_cols, 128, field_b[...]) + pick(edge_cols, 128, field_l[...])
         remote(y_out, y_in.at[par, 1], halo_send_sem.at[2], halo.at[3], at(0, -1)).start()
         remote(y_out, y_in.at[par, 0], halo_send_sem.at[3], halo.at[2], at(0, 1)).start()
+
+        pl.when(step == 1)(tangents)
 
         for side in range(2):
             pltpu.make_async_copy(x_in.at[par, side], x_in.at[par, side], halo.at[side]).wait()
@@ -249,12 +338,8 @@
                     lane < rx, y_in[par, 1] * right_ok, y_in[par, 0] * left_ok
                 )
             got = got * wrow[:, cols]
-            mask = put_x[:, cols]
-            for c in range(6):
-                r = c + c // 3
-                spread[c * rx : (c + 1) * rx, cols] = mask * jnp.broadcast_to(
-                    got[r : r + 1].astype(BF16), (rx, 128)
-                )
+            scatter(got, t * 128, put_x[:, cols])
+        scatter(got - got.astype(BF16).astype(F32), slots + 128, put_x[:, cols])
         coupled = jnp.dot(spread[...], put_y[...], preferred_element_type=F32)
 
         pltpu.make_async_copy(msg_out.at[most], msg_out.at[most], msg_send_sem).wait()
@@ -263,49 +348,121 @@
             pltpu.make_async_copy(y_out, y_out, halo_send_sem.at[2 + side]).wait()
 
         st = stiff_s[...]
-        lane_w = lax.broadcasted_iota(jnp.int32, (rx, ry), 1)
-        sub_w = lax.broadcasted_iota(jnp.int32, (rx, ry), 0)
 
         def h(c):
             f = field[c]
-            above = jnp.broadcast_to(x_in[par, 0, c : c + 1, :] * up_ok, (rx, ry))
-            below = jnp.broadcast_to(x_in[par, 1, c : c + 1, :] * down_ok, (rx, ry))
-            nb = jnp.where(sub_w == 0, above, pltpu.roll(f, 1, 0))
-            nb += jnp.where(sub_w == rx - 1, below, pltpu.roll(f, rx - 1, 0))
-            nb += jnp.where(lane_w == 0, 0.0, pltpu.roll(f, 1, 1))
-            nb += jnp.where(lane_w == ry - 1, 0.0, pltpu.roll(f, ry - 1, 1))
+            nb = across_x(
+                f, x_in[par, 0, c : c + 1, :] * up_ok, x_in[par, 1, c : c + 1, :] * down_ok
+            )
+            nb += across_y(f, 0.0, 0.0)
             return rhs_ref[c] + st * nb + coupled[c * rx : (c + 1) * rx]
 
         update(h)
         return carry
 
     lax.fori_loop(1, ITERS, sweep, 0)
+
+    sens = jnp.zeros((rx, ry), F32)
+    for c in range(3):
+        sens += field[c] * tangent[c] - field[c + 3] * tangent[c + 3]
+    mine = -sens * dens_ref[...]
+    sens_out[...] = mine
+    sens_in[fr, :, :] = mine
+    edge_out[0, :, :] = mine[:1, :128]
+    edge_out[1, :, :] = mine[:1, ry - 128 :]
+    edge_out[2, :, :] = mine[rx - 1 :, :128]
+    edge_out[3, :, :] = mine[rx - 1 :, ry - 128 :]
+    eye_l = onehot(sub_x, lane_row)
+    eye_h = onehot(sub_x, lane_row - rx)
+    edge_out[4, :, :] = jnp.sum(
+        mine[:, :1] * eye_l + mine[:, ry - 1 :] * eye_h, axis=0, keepdims=True
+    )
+    routes = [
+        (-1, 0, 0, 2, 2),
+        (1, 0, 2, 0, 2),
+        (0, -1, 4, 5, 1),
+        (0, 1, 4, 4, 1),
+        (-1, -1, 0, 6, 1),
+        (-1, 1, 1, 7, 1),
+        (1, -1, 2, 8, 1),
+        (1, 1, 3, 9, 1),
+    ]
+    for df in range(n_freq):
+        for a, b, src, dst, size in routes:
+            remote(
+                edge_out.at[pl.ds(src, size)],
+                edge_in.at[fr, pl.ds(dst, size)],
+                edge_send_sem,
+                edge_recv_sem,
+                at(a, b, df),
+            ).start()
+    for df in range(1, n_freq):
+        remote(sens_out, sens_in.at[fr], sens_send_sem, sens_recv_sem, at(0, 0, df)).start()
     out_ref[...] = field[...]
-
-
-def solve(n_mx, n_my, rhs, density, stiffness, mass, omega, send_rows, recv_rows, mortar_weight):
+    pltpu.make_async_copy(edge_in, edge_in, edge_recv_sem).wait()
+    total_edge = [edge_in[0, k] for k in range(10)]
+    for f in range(1, n_freq):
+        total_edge = [total_edge[k] + edge_in[f, k] for k in range(10)]
+    above = jnp.concatenate(total_edge[0:2], axis=1) * up_ok
+    below = jnp.concatenate(total_edge[2:4], axis=1) * down_ok
+    sides = jnp.where(low, total_edge[5] * right_ok, total_edge[4] * left_ok)
+    down_right = total_edge[6][:, :1] * (down_ok * right_ok)
+    down_left = total_edge[7][:, 127:] * (down_ok * left_ok)
+    up_right = total_edge[8][:, :1] * (up_ok * right_ok)
+    up_left = total_edge[9][:, 127:] * (up_ok * left_ok)
+    before = jnp.where(
+        lane_row == 0, up_right, jnp.where(lane_row == rx, up_left, pltpu.roll(sides, 1, 1))
+    )
+    after = jnp.where(
+        lane_row == rx - 1,
+        down_right,
+        jnp.where(lane_row == 2 * rx - 1, down_left, pltpu.roll(sides, 127, 1)),
+    )
+    sides = sides + 0.5 * (before + after)
+    col_right = jnp.sum(eye_l * sides, axis=1, keepdims=True)
+    col_left = jnp.sum(eye_h * sides, axis=1, keepdims=True)
+    others = pl.ds(0, n_freq - 1)
+    pltpu.make_async_copy(sens_in.at[others], sens_in.at[others], sens_recv_sem).wait()
+    total = sens_in[0]
+    for f in range(1, n_freq):
+        total += sens_in[f]
+    total = total + 0.5 * across_x(total, above, below)
+    total = total + 0.5 * across_y(total, col_left, col_right)
+    filt_ref[...] = total / (4.0 * dens_ref[...])
+    pltpu.make_async_copy(edge_in, edge_in, edge_send_sem).wait()
+    pltpu.make_async_copy(sens_in.at[others], sens_in.at[others], sens_send_sem).wait()
+
+
+def on_device(
+    adjoint_rhs, state, density, stiffness, mass, omega, send_rows, recv_rows, mortar_weight
+):
     rx, ry = density.shape
     slots = send_rows.shape[1]
     wide = slots + 128
+    n_freq, n_mx, n_my = (lax.axis_size(name) for name in ("freq", "mx", "my"))
     peers = n_mx * n_my
     vmem = pl.BlockSpec(memory_space=pltpu.VMEM)
-    return pl.pallas_call(
-        functools.partial(sweeps_kernel, n_mx, n_my),
-        out_shape=jax.ShapeDtypeStruct((6, rx, ry), F32),
-        in_specs=[vmem] * 4 + [pl.BlockSpec(memory_space=pltpu.SMEM)] + [vmem] * 3,
-        out_specs=vmem,
+    field, filtered = pl.pallas_call(
+        functools.partial(sweeps_kernel, n_freq, n_mx, n_my),
+        out_shape=(
+            jax.ShapeDtypeStruct((6, rx, ry), F32),
+            jax.ShapeDtypeStruct((rx, ry), F32),
+        ),
+        in_specs=[vmem] * 5 + [pl.BlockSpec(memory_space=pltpu.SMEM)] + [vmem] * 3,
+        out_specs=(vmem, vmem),
         scratch_shapes=[
             pltpu.VMEM((6, rx, ry), F32),
+            pltpu.VMEM((6 * rx, ry), BF16),
             pltpu.VMEM((6 * rx, ry), BF16),
             pltpu.VMEM((rx, ry), F32),
             pltpu.VMEM((rx, ry), F32),
             pltpu.VMEM((rx, ry), F32),
             pltpu.VMEM((ry, wide), BF16),
             pltpu.VMEM((rx, wide), F32),
-            pltpu.VMEM((wide, ry), BF16),
+            pltpu.VMEM((wide + 128, ry), BF16),
             pltpu.VMEM((rx, wide), BF16),
             pltpu.VMEM((1, wide), F32),
-            pltpu.VMEM((6 * rx, wide), BF16),
+            pltpu.VMEM((6 * rx, wide + 128), BF16),
             pltpu.VMEM((peers, 2, 128), BF16),
             pltpu.VMEM((2, peers, 2, 128), BF16),
             pltpu.VMEM((8, 128), F32),
@@ -317,59 +474,35 @@
             pltpu.SemaphoreType.DMA,
             pltpu.SemaphoreType.DMA((4,)),
             pltpu.SemaphoreType.DMA((2, 4)),
+            pltpu.VMEM((6, rx, ry), F32),
+            pltpu.VMEM((2, 8, ry), F32),
+            pltpu.VMEM((2, 8, ry), F32),
+            pltpu.VMEM((8, 128), F32),
+            pltpu.VMEM((2, 8, 128), F32),
+            pltpu.SemaphoreType.DMA((4,)),
+            pltpu.SemaphoreType.DMA((4,)),
+            pltpu.VMEM((rx, ry), F32),
+            pltpu.VMEM((n_freq, rx, ry), F32),
+            pltpu.VMEM((5, 1, 128), F32),
+            pltpu.VMEM((n_freq, 10, 1, 128), F32),
+            pltpu.SemaphoreType.DMA,
+            pltpu.SemaphoreType.DMA,
+            pltpu.SemaphoreType.DMA,
+            pltpu.SemaphoreType.DMA,
         ],
         compiler_params=pltpu.CompilerParams(collective_id=0, has_side_effects=True),
-    )(rhs, density, stiffness, mass, omega, send_rows, recv_rows, mortar_weight)
-
-
-def extended(x, sides, width):
-    for axis, dim in sides:
-        size, length = (lax.axis_size(axis), x.shape[dim])
-        up = [(i, (i + 1) % size) for i in range(size - 1)]
-        down = [(j, i) for i, j in up]
-        last = lax.slice_in_dim(x, length - width, length, axis=dim)
-        first = lax.slice_in_dim(x, 0, width, axis=dim)
-        before = lax.ppermute(last, axis, up)
-        after = lax.ppermute(first, axis, down)
-        x = jnp.concatenate([before, x, after], axis=dim)
-    return x
-
-
-def on_device(
-    adjoint_rhs, state, density, stiffness, mass, omega, send_rows, recv_rows, mortar_weight
-):
-    rows_x, rows_y = density.shape
-    w = omega[0]
-    dstiff = 3.0 * density**2 * stiffness
-    rhs = adjoint_rhs.reshape(6, rows_x, rows_y)
-    field = solve(
-        lax.axis_size("mx"), lax.axis_size("my"),
-        rhs, density, stiffness, mass, omega, send_rows, recv_rows, mortar_weight,
+    )(
+        adjoint_rhs.reshape(6, rx, ry),
+        state.reshape(6, rx, ry),
+        density,
+        stiffness,
+        mass,
+        omega,
+        send_rows,
+        recv_rows,
+        mortar_weight,
     )
-    state_six = state.reshape(6, rows_x, rows_y)
-    state_pad = extended(state_six, (("mx", 1), ("my", 2)), 1).astype(jnp.float32)
-    u = state_six.astype(jnp.float32)
-    nb = (
-        state_pad[:, 2:, 1:-1]
-        + state_pad[:, :-2, 1:-1]
-        + state_pad[:, 1:-1, 2:]
-        + state_pad[:, 1:-1, :-2]
-    )
-    da = 4.4 * dstiff - w * w * mass
-    db = 0.2 * w * (dstiff + mass)
-    t_re = da * u[:3] - db * u[3:] - dstiff * nb[:3]
-    t_im = da * u[3:] + db * u[:3] - dstiff * nb[3:]
-    sens = -jnp.sum(field[:3] * t_re - field[3:] * t_im, axis=0)
-    total = lax.psum(sens, "freq")
-    weighted = extended(density * total, (("mx", 0), ("my", 1)), 1)
-    filt = weighted[1:-1, 1:-1]
-    filt = filt + 0.5 * (
-        weighted[2:, 1:-1] + weighted[:-2, 1:-1] + weighted[1:-1, 2:] + weighted[1:-1, :-2]
-    )
-    filt = filt + 0.25 * (
-        weighted[2:, 2:] + weighted[:-2, :-2] + weighted[2:, :-2] + weighted[:-2, 2:]
-    )
-    return (field.reshape(1, 2, 3, rows_x, rows_y), filt / (4.0 * density))
+    return field.reshape(1, 2, 3, rx, ry), filtered
 
 
 def solution(mesh):

time: 265 us -> 172 us (0.65)
  waiting for transfers between devices: 47.3 us -> 0 us
  starting transfers between devices: 24.3 us -> 0 us
  between operations: 14.9 us -> 1.29 us
  other arithmetic: 4.13 us -> 0 us
    psum x1 -> x0, waiting for transfers between devices: 44.2 us -> none  [on_device(): total = lax.psum(sens, 'freq')]
    ppermute x8 -> x0, starting transfers between devices: 24.2 us -> none  [the longest x4 15 us: extended(): before = lax.ppermute(last, axis, up)]
    ppermute x8 -> x0, waiting for transfers between devices: 3.04 us -> none  [the longest x4 1.69 us: extended(): before = lax.ppermute(last, axis, up)]
  transfers between devices with their start and end apart: 9 -> 0, of which waited for: 5 -> 0; matrix products, arithmetic and copies ran while one was open for 0% -> 0% of each run, Pallas kernels for 65% -> 0%
where the time goes in v2:
time: 172 us; the launch traced here: 171 us
  Pallas kernels  168 us (98%)
  local copies, waits for them, and re-layouts  2.44 us (1%)
    pallas_call x1, Pallas kernels, on_device(): pl.pallas_call(functools.partial(sweeps_kernel, n_freq, n_mx, n_my), out_...  168 us

profile of v2, /device:TPU:1, one launch (start us, length us, event | category | flops | bytes accessed | tf_op | source)
XLA Modules:
  0.0 171.4 jit_solution(18256122051716656721)
XLA Ops:
  1.3 167.7 %shard_map.104 = (f32[6,64,256]{2,1,0:T(8,128)}, f32[64,256]{1,0:T(8,128)}) custom-call(f32[6,64,256]{2,1,0:T(8,128)} %bitcast.4, bf16[6,64,256]{2,1,0:T(8,128)(2,1)} %bitcast.5, f32[64,256]{1,0:T(8,128)} %dens_ref.1, f32[64,256]{1,0:T(8,128)} %stiffness_ref.1, f32[64,256]{1,0:T(8,128)} %mass_ref.1, f32[1]{0:T(128)S(6)} %copy.13.omega_ref, ...), custom_call_target="tpu_custom_call" | custom-call | tf_op jit(solution)/shard_map/pallas_call | solution.py:445
  169.0 0.0 copy-start
  169.0 1.8 %copy.14 = f32[1,2,3,64,256]{4,3,2,1,0:T(8,128)} copy(f32[1,2,3,64,256]{4,3,2,1,0:T(8,128)} %bitcast.3) | data formatting | bytes 786432
  170.8 0.0 copy-done
  170.8 0.6 copy.15
Async XLA Ops:
  169.0 1.8 %copy-start = (f32[64,256]{1,0:T(8,128)S(1)}, f32[64,256]{1,0:T(8,128)}, u32[]{:S(2)}) copy-start(f32[64,256]{1,0:T(8,128)} %get-tuple-element.9) | copy-start | bytes 196612

commit v3 on v2

--- a/solution.py
+++ b/solution.py
@@ -8,6 +8,7 @@
 from jax.sharding import PartitionSpec as P
 
 ITERS = 20
+FAR = 3
 MESH = pl.DeviceIdType.MESH
 F32 = jnp.float32
 BF16 = jnp.bfloat16
@@ -70,6 +71,10 @@
     sens_recv_sem,
     edge_send_sem,
     edge_recv_sem,
+    send_by,
+    recv_by,
+    weight_by,
+    part,
 ):
     fr = lax.axis_index("freq")
     i = lax.axis_index("mx")
@@ -87,13 +92,9 @@
             "my": lax.rem(j + dj + n_my, n_my),
         }
 
-    offsets = [(a, b) for a in range(n_mx) for b in range(n_my) if a or b]
-
-    def far(o):
-        a, b = o
-        return -(min(b, n_my - b) + min(a, n_mx - a) / 2.0)
-
-    offsets.sort(key=far)
+    order_x = sorted(range(n_mx), key=lambda a: -min(a, n_mx - a))
+    order_y = sorted(range(n_my), key=lambda b: -min(b, n_my - b))
+    offsets = [(a, b) for b in order_y for a in order_x if a or b]
 
     barrier = pltpu.get_barrier_semaphore()
     for a, b in offsets:
@@ -121,11 +122,40 @@
     lane_y = lax.broadcasted_iota(jnp.int32, (128, ry), 1)
     lane_row = lax.broadcasted_iota(jnp.int32, (1, 128), 1)
     low = lane_row < rx
+
+    def regroup(row_ref, to_ref):
+        per = n_my // 4
+        for g in range(n_mx // 4):
+            parts = None
+            for turn in range(4):
+                picked = [
+                    row_ref[:, pl.ds(((4 * g + (d + turn) % 4) * per + h) * 128, 128)]
+                    for h in range(per)
+                    for d in range(4)
+                ]
+                r = jnp.concatenate(picked, axis=0)
+                if turn:
+                    r = pltpu.roll(r, 32 * turn, 1)
+                r = jnp.where(block == lax.bitwise_and(comp + turn, 3), r, jnp.zeros_like(r))
+                parts = r if parts is None else parts + r
+            for y in range(n_my):
+                to_ref[y, :, g * 128 : (g + 1) * 128] = parts[y : y + 1]
+
+    regroup(send_ref, send_by)
+    regroup(recv_ref, recv_by)
+    regroup(weight_ref, weight_by)
+    run = n_mx * 32
+    for n, b in enumerate(order_y):
+        j_from = lax.rem(j - b + n_my, n_my)
+        wrow[:, n * run : (n + 1) * run] = weight_by[j_from]
     for t in range(tiles + 1):
         cols = slice(t * 128, (t + 1) * 128)
         if t < tiles:
-            src = send_ref[:, cols]
-            dst = recv_ref[:, cols]
+            n, g = divmod(t * 128, run)
+            j_to = lax.rem(j + order_y[n], n_my)
+            j_from = lax.rem(j - order_y[n] + n_my, n_my)
+            src = send_by[j_to, :, g : g + 128]
+            dst = recv_by[j_from, :, g : g + 128]
             sx, sy = lax.shift_right_logical(src, 8), lax.bitwise_and(src, ry - 1)
             dx, dy = lax.shift_right_logical(dst, 8), lax.bitwise_and(dst, ry - 1)
         else:
@@ -138,14 +168,13 @@
         turned = jnp.broadcast_to(dy.astype(F32), (128, 128)).T.astype(jnp.int32)
         put_y[cols, :] = onehot(lane_y, jnp.concatenate([turned] * (ry // 128), axis=1)).astype(BF16)
     put_y[slots + 128 :, :] = put_y[slots : slots + 128, :]
-    wrow[:, :slots] = weight_ref[...]
     eye_low = onehot(sub_x, lane_row)
     eye_high = onehot(sub_x, lane_row - rx)
     wrow[:, slots:] = jnp.sum(
         stiff[:, ry - 1 :] * eye_low + stiff[:, :1] * eye_high, axis=0, keepdims=True
     )
 
-    whole = weight_ref[...]
+    whole = wrow[:, :slots]
     hi = whole.astype(BF16)
     rest = whole - hi.astype(F32)
     mid = rest.astype(BF16)
@@ -259,16 +288,25 @@
     def sweep(step, carry):
         par = lax.rem(step, 2)
 
-        for c in range(6):
-            x_out[0, c : c + 1, :] = field[c, 0:1, :]
-            x_out[1, c : c + 1, :] = field[c, rx - 1 : rx, :]
         halo = halo_recv_sem.at[par]
-        remote(x_out.at[0], x_in.at[par, 1], halo_send_sem.at[0], halo.at[1], at(-1, 0)).start()
-        remote(x_out.at[1], x_in.at[par, 0], halo_send_sem.at[1], halo.at[0], at(1, 0)).start()
-
-        for t in range(tiles // 2):
-            rows = pick(slice(t * 256, (t + 1) * 256), 256, field_b[...])
-            for half in range(2):
+
+        own = pltpu.make_async_copy(
+            msg_out.at[(n_my - 1) * n_mx + i], msg_in.at[par, n_my - 1, i], own_sem
+        )
+        for n, b in enumerate(order_y):
+            if n == FAR:
+                for c in range(6):
+                    x_out[0, c : c + 1, :] = field[c, 0:1, :]
+                    x_out[1, c : c + 1, :] = field[c, rx - 1 : rx, :]
+                remote(x_out.at[0], x_in.at[par, 1], halo_send_sem.at[0], halo.at[1], at(-1, 0)).start()
+                remote(x_out.at[1], x_in.at[par, 0], halo_send_sem.at[1], halo.at[0], at(1, 0)).start()
+
+                y_out[...] = pick(edge_cols, 128, field_b[...]) + pick(edge_cols, 128, field_l[...])
+                remote(y_out, y_in.at[par, 1], halo_send_sem.at[2], halo.at[3], at(0, -1)).start()
+                remote(y_out, y_in.at[par, 0], halo_send_sem.at[3], halo.at[2], at(0, 1)).start()
+
+            rows = pick(slice(n * run, (n + 1) * run), run, field_b[...])
+            for half in range(n_mx // 4):
                 r = rows[:, half * 128 : (half + 1) * 128]
                 x = jnp.where(
                     comp == 1, pltpu.roll(r, 32, 1), jnp.where(comp == 2, pltpu.roll(r, 64, 1), r)
@@ -283,40 +321,33 @@
                         ],
                         axis=0,
                     )
-                    msg_out[(2 * t + half) * 4 + d] = m.astype(BF16)
-        own = pltpu.make_async_copy(msg_out.at[me], msg_in.at[par, me], own_sem)
-        own.start()
-        for a, b in offsets:
-            to = at(a, b)
-            remote(
-                msg_out.at[to["mx"] * n_my + to["my"]],
-                msg_in.at[par, me],
-                msg_send_sem,
-                msg_recv_sem.at[par],
-                to,
-            ).start()
-
-        y_out[...] = pick(edge_cols, 128, field_b[...]) + pick(edge_cols, 128, field_l[...])
-        remote(y_out, y_in.at[par, 1], halo_send_sem.at[2], halo.at[3], at(0, -1)).start()
-        remote(y_out, y_in.at[par, 0], halo_send_sem.at[3], halo.at[2], at(0, 1)).start()
+                    msg_out[n * n_mx + half * 4 + d] = m.astype(BF16)
+            for a in order_x:
+                if a or b:
+                    to = at(a, b)
+                    remote(
+                        msg_out.at[n * n_mx + to["mx"]],
+                        msg_in.at[par, n, i],
+                        msg_send_sem,
+                        msg_recv_sem.at[par, n],
+                        to,
+                    ).start()
+                else:
+                    own.start()
 
         pl.when(step == 1)(tangents)
 
-        for side in range(2):
-            pltpu.make_async_copy(x_in.at[par, side], x_in.at[par, side], halo.at[side]).wait()
-            pltpu.make_async_copy(y_in.at[par, side], y_in.at[par, side], halo.at[2 + side]).wait()
-        own.wait()
-        most = pl.ds(0, peers - 1)
-        pltpu.make_async_copy(
-            msg_in.at[par, most], msg_in.at[par, most], msg_recv_sem.at[par]
-        ).wait()
-
-        for t in range(tiles + 1):
-            cols = slice(t * 128, (t + 1) * 128)
-            if t < tiles:
+        def arrived(n):
+            if order_y[n]:
+                group = msg_in.at[par, n]
+            else:
+                own.wait()
+                group = msg_in.at[par, n, pl.ds(0, n_mx - 1)]
+            pltpu.make_async_copy(group, group, msg_recv_sem.at[par, n]).wait()
+            for half in range(n_mx // 4):
                 got = None
                 for d in range(4):
-                    m = msg_in[par, 4 * t + d].astype(F32)
+                    m = msg_in[par, n, 4 * half + d].astype(F32)
                     u = jnp.concatenate(
                         [
                             jnp.broadcast_to(m[0:1], (4, 128)),
@@ -333,31 +364,43 @@
                     pltpu.roll(got, 96, 1),
                     jnp.where(comp == 2, pltpu.roll(got, 64, 1), got),
                 )
-            else:
-                got = jnp.where(
-                    lane < rx, y_in[par, 1] * right_ok, y_in[par, 0] * left_ok
-                )
-            got = got * wrow[:, cols]
-            scatter(got, t * 128, put_x[:, cols])
-        scatter(got - got.astype(BF16).astype(F32), slots + 128, put_x[:, cols])
-        coupled = jnp.dot(spread[...], put_y[...], preferred_element_type=F32)
-
-        pltpu.make_async_copy(msg_out.at[most], msg_out.at[most], msg_send_sem).wait()
+                start = n * run + half * 128
+                cols = slice(start, start + 128)
+                scatter(got * wrow[:, cols], start, put_x[:, cols])
+
         for side in range(2):
-            pltpu.make_async_copy(x_out.at[side], x_out.at[side], halo_send_sem.at[side]).wait()
-            pltpu.make_async_copy(y_out, y_out, halo_send_sem.at[2 + side]).wait()
-
+            pltpu.make_async_copy(x_in.at[par, side], x_in.at[par, side], halo.at[side]).wait()
+            pltpu.make_async_copy(y_in.at[par, side], y_in.at[par, side], halo.at[2 + side]).wait()
+        got = jnp.where(lane < rx, y_in[par, 1] * right_ok, y_in[par, 0] * left_ok)
+        got = got * wrow[:, edge_cols]
+        scatter(got, slots, put_x[:, edge_cols])
+        scatter(got - got.astype(BF16).astype(F32), slots + 128, put_x[:, edge_cols])
+        for n in range(n_my - 1, FAR - 1, -1):
+            arrived(n)
+        near = jnp.dot(
+            spread[:, FAR * run :], put_y[FAR * run :, :], preferred_element_type=F32
+        )
         st = stiff_s[...]
-
-        def h(c):
+        for c in range(6):
             f = field[c]
             nb = across_x(
                 f, x_in[par, 0, c : c + 1, :] * up_ok, x_in[par, 1, c : c + 1, :] * down_ok
             )
             nb += across_y(f, 0.0, 0.0)
-            return rhs_ref[c] + st * nb + coupled[c * rx : (c + 1) * rx]
-
-        update(h)
+            part[c, :, :] = rhs_ref[c] + st * nb + near[c * rx : (c + 1) * rx]
+
+        most = pl.ds(0, peers - 1)
+        pltpu.make_async_copy(msg_out.at[most], msg_out.at[most], msg_send_sem).wait()
+        for side in range(2):
+            pltpu.make_async_copy(x_out.at[side], x_out.at[side], halo_send_sem.at[side]).wait()
+            pltpu.make_async_copy(y_out, y_out, halo_send_sem.at[2 + side]).wait()
+
+        for n in range(FAR - 1, -1, -1):
+            arrived(n)
+        distant = jnp.dot(
+            spread[:, : FAR * run], put_y[: FAR * run, :], preferred_element_type=F32
+        )
+        update(lambda c: part[c] + distant[c * rx : (c + 1) * rx])
         return carry
 
     lax.fori_loop(1, ITERS, sweep, 0)
@@ -464,13 +507,13 @@
             pltpu.VMEM((1, wide), F32),
             pltpu.VMEM((6 * rx, wide + 128), BF16),
             pltpu.VMEM((peers, 2, 128), BF16),
-            pltpu.VMEM((2, peers, 2, 128), BF16),
+            pltpu.VMEM((2, n_my, n_mx, 2, 128), BF16),
             pltpu.VMEM((8, 128), F32),
             pltpu.VMEM((2, 2, 8, 128), F32),
             pltpu.VMEM((2, 8, ry), F32),
             pltpu.VMEM((2, 2, 8, ry), F32),
             pltpu.SemaphoreType.DMA,
-            pltpu.SemaphoreType.DMA((2,)),
+            pltpu.SemaphoreType.DMA((2, n_my)),
             pltpu.SemaphoreType.DMA,
             pltpu.SemaphoreType.DMA((4,)),
             pltpu.SemaphoreType.DMA((2, 4)),
@@ -489,6 +532,10 @@
             pltpu.SemaphoreType.DMA,
             pltpu.SemaphoreType.DMA,
             pltpu.SemaphoreType.DMA,
+            pltpu.VMEM((n_my, 1, n_mx * 32), jnp.int32),
+            pltpu.VMEM((n_my, 1, n_mx * 32), jnp.int32),
+            pltpu.VMEM((n_my, 1, n_mx * 32), F32),
+            pltpu.VMEM((6, rx, ry), F32),
         ],
         compiler_params=pltpu.CompilerParams(collective_id=0, has_side_effects=True),
     )(

time: 172 us -> 210 us (1.22)
  Pallas kernels: 168 us -> 206 us
    pallas_call x1, Pallas kernels: 168 us -> 206 us  [on_device(): pl.pallas_call(functools.partial(sweeps_kernel, n_freq, n_mx, n_my), out_...]
where the time goes in v3:
time: 210 us
  Pallas kernels  206 us (98%)
  local copies, waits for them, and re-layouts  2.44 us (1%)
    pallas_call x1, Pallas kernels, on_device(): pl.pallas_call(functools.partial(sweeps_kernel, n_freq, n_mx, n_my), out_...  206 us

profile of v3, /device:TPU:1, one launch (start us, length us, event | category | flops | bytes accessed | tf_op | source)
XLA Modules:
  0.0 209.7 jit_solution(5708342468119707634)
XLA Ops:
  1.3 206.0 %shard_map.104 = (f32[6,64,256]{2,1,0:T(8,128)}, f32[64,256]{1,0:T(8,128)}) custom-call(f32[6,64,256]{2,1,0:T(8,128)} %bitcast.4, bf16[6,64,256]{2,1,0:T(8,128)(2,1)} %bitcast.5, f32[64,256]{1,0:T(8,128)} %dens_ref.1, f32[64,256]{1,0:T(8,128)} %stiffness_ref.1, f32[64,256]{1,0:T(8,128)} %mass_ref.1, f32[1]{0:T(128)S(6)} %copy.13.omega_ref, ...), custom_call_target="tpu_custom_call" | custom-call | tf_op jit(solution)/shard_map/pallas_call | solution.py:488
  207.3 0.0 copy-start
  207.3 1.8 copy.14
  209.1 0.0 copy-done
  209.1 0.6 copy.15
Async XLA Ops:
  207.3 1.8 copy-start
